TPU v7x, 256 devices: a whole 4x4x8 slice. The times are simulated.
256 devices in a mesh: seq: 32 (over y_hi, z, core), head: 8 (over y_lo, x).
Axes of the slice: x: 4, y: 4 (y_hi: 2, y_lo: 2; y = y_hi * 2 + y_lo), z: 8, core: 2. Of those that a mesh axis runs over, the one named last changes fastest.
Arguments:
- queries: bfloat16 [4096, 8192], P('seq', 'head'), may hold values from -190 to 190
- key_vectors: bfloat16 [4096, 1024], P('seq', 'head'), may hold values from -6.1 to 6.1
- value_vectors: bfloat16 [4096, 1024], P('seq', 'head'), may hold values from -54 to 54
- log_gate: float32 [64, 4096], P('head', 'seq'), may hold values from -1 to 0, as said below
- query_map: float32 [64, 128, 128], P('head'), may hold values from -0.5 to 0.5
- key_map: float32 [64, 128, 128], P('head'), may hold values from -0.5 to 0.5
- level_weight: float32 [64, 13], P('head'), may hold values from 0.25 to 2
- norm_gain: float32 [8192], P('head'), may hold values from 0.5 to 1.5
Outputs:
- grad_query_map: float32 [64, 128, 128], P('head')
- grad_key_map: float32 [64, 128, 128], P('head')
- grad_level_weight: float32 [64, 13], P('head')
- grad_norm_gain: float32 [8192], P('head')
Inputs may be any that keep to these rules, and one draw needn't show every extreme that they name: `log_gate`: every entry is negative.
All inputs are finite; a program needn't handle non-finite values.
Results may differ from a plain program's by a relative error of at most 0.0015.
Values may be sent and summed in bfloat16 or wider, within the bound.
A program may use at most 128 MiB of HBM per device.

v0:
```python
import jax
import jax.numpy as jnp
from jax import lax
from jax.experimental import pallas as pl
from jax.experimental.pallas import tpu as pltpu
from jax.sharding import PartitionSpec as P

F32 = jnp.float32
BF = jnp.bfloat16
HIGHEST = lax.Precision.HIGHEST
MESH = pl.DeviceIdType.MESH
NEGATIVE = -1e30
EPSILON = 1e-05
HD = 128
TOK = 128
HEADS = 8
SPANS = 32
LEVELS = 13
LOW = 7
CROSS = 5
TOKENS = TOK * SPANS
WIDTH = 64 * HD
SMALL = 24
HALF = HD // 2
LOG2E = 1.4426950408889634
SCALE = HD**-0.5 * LOG2E
LIMIT = 58 << 20


def pieces(a):
    high = a.astype(BF)
    return high, (a - high.astype(F32)).astype(BF)


def dg(a, b, ca, cb, precision=None):
    return lax.dot_general(
        a, b, (((ca,), (cb,)), ((), ())), preferred_element_type=F32, precision=precision
    )


def halves(o):
    n = o.shape[1] // 2
    return o[:, :n] + o[:, n:]


def mm(a, b, ca, cb):
    bh, bl = pieces(b)
    left = jnp.concatenate(pieces(a), axis=ca)
    right = jnp.concatenate(
        [jnp.concatenate([bh, bh], axis=cb), jnp.concatenate([bl, bl], axis=cb)], axis=1 - cb
    )
    return halves(dg(left, right, ca, cb))


def mm_left_exact(a, b, ca, cb):
    return halves(dg(a, jnp.concatenate(pieces(b), axis=1 - cb), ca, cb))


def mm_right_exact(a, b, ca, cb):
    return dg(jnp.concatenate(pieces(a), axis=ca), jnp.concatenate([b, b], axis=cb), ca, cb)


def iota(shape, dim):
    return lax.broadcasted_iota(jnp.int32, shape, dim)


def local_levels():
    x = jnp.bitwise_xor(iota((TOK, TOK), 0), iota((TOK, TOK), 1))
    level = jnp.zeros_like(x)
    for bit in range(LOW):
        level = level + (x >= 1 << bit).astype(jnp.int32)
    return level


def rows(h):
    return slice(h * TOK, (h + 1) * TOK)


def column_cumulative(gates):
    lower = (iota((TOK, TOK), 1) <= iota((TOK, TOK), 0)).astype(F32)
    return dg(lower, gates, 1, 1, HIGHEST)


def pair_of(kv, which, p):
    return kv[which, pl.ds(2 * p, 2)].reshape(2 * TOK, HD)


def scored(c, p, masked, qs, kv, peak, score):
    keys = pair_of(kv, 0, p)
    for h in range(HEADS):
        s = dg(qs[rows(h)], keys, 1, 1)
        if masked:
            place_of = 2 * TOK * p + iota((TOK, 2 * TOK), 1)
            s = jnp.where(place_of <= c * TOK + iota((TOK, 2 * TOK), 0), s, NEGATIVE)
        score[p, rows(h)] = s
        top = jnp.maximum(s[:, :TOK], s[:, TOK:])
        peak[rows(h)] = top if masked else jnp.maximum(peak[rows(h)], top)


def weighed(p, h, values, score, peak, total, tgt):
    s = score[p, rows(h)]
    top = peak[rows(h)]
    w0 = jnp.exp2((s[:, :TOK] - top) * SCALE)
    w1 = jnp.exp2((s[:, TOK:] - top) * SCALE)
    total[rows(h)] += w0 + w1
    tgt[h] += dg(jnp.concatenate([w0.astype(BF), w1.astype(BF)], axis=1), values, 1, 0)


def level_weights(c, gates, lc, weights):
    upper = (iota((TOK, TOK), 0) <= iota((TOK, TOK), 1)).astype(F32)
    lc[...] = dg(gates[...].reshape(SPANS * HEADS, TOK), upper, 1, 0, HIGHEST)

    def step(i, since):
        x = c - 1 - i
        own = lc[pl.ds(pl.multiple_of(x * HEADS, HEADS), HEADS)]
        since = since + own[:, TOK - 1 :]
        weights[x] = jnp.exp(since - own)
        return since

    lax.fori_loop(0, c, step, jnp.zeros((HEADS, 1), F32))


def student_inside(qs, kv, c, gate, wq, wk, lw, qp, kp, mix, sd):
    key = kv[0, c]
    upper = (iota((TOK, TOK), 0) <= iota((TOK, TOK), 1)).astype(F32)
    row_cum = dg(gate, upper, 1, 0, HIGHEST)
    col_cum = column_cumulative(gate)
    causal = iota((TOK, TOK), 1) <= iota((TOK, TOK), 0)
    level = local_levels()
    for h in range(HEADS):
        qp[h] = mm_left_exact(qs[rows(h)], wq[h], 1, 0)
        kp[h] = mm_left_exact(key, wk[h], 1, 0)
    for h in range(HEADS):
        decay = jnp.exp(
            jnp.where(causal, col_cum[:, h : h + 1] - row_cum[h : h + 1], NEGATIVE)
        )
        mask = jnp.full((TOK, TOK), lw[h, 0], F32)
        for j in range(1, LOW + 1):
            mask = jnp.where(level == j, lw[h, j], mask)
        sd[h] = mm(qp[h], kp[h], 1, 1) * decay
        mix[h] = decay * mask


def student_whole(entry, kv, c, wk, lw, gain, ls, tgt, qp, ks, comb, raw, local):
    for h in range(HEADS):
        combined = lw[h, LOW + 1] * ls[0, h]
        for j in range(1, CROSS):
            combined = combined + lw[h, LOW + 1 + j] * ls[j, h]
        comb[h] = combined
        ks[h] = mm(wk[h], combined, 0, 0)
    square = jnp.zeros((TOK, HD), F32)
    scaled = jnp.zeros((TOK, HD), F32)
    against = jnp.zeros((TOK, HD), F32)
    for h in range(HEADS):
        r = local[h] + entry[:, h : h + 1] * mm(qp[h], ks[h], 1, 0)
        raw[h] = r
        rg = r * gain[h : h + 1]
        square = square + r * r
        scaled = scaled + rg * rg
        against = against + tgt[h] * rg
    one = jnp.ones((8, HD), F32)
    tile = [dg(one, x, 1, 1, HIGHEST) for x in (square, scaled, against)]
    return jnp.concatenate([t[:1] for t in tile] + [tile[0][:5]], axis=0)


def backward_inside(
    all_sums, entry, kv, c, wk, gain, ls, tgt, qp, kp, ks, comb, mix, sd, raw, res, dstate, dquery, dkey
):
    value = kv[1, c]
    eye = (iota((TOK, TOK), 0) == iota((TOK, TOK), 1)).astype(F32)
    level = local_levels()
    column = dg(eye, all_sums, 1, 1, HIGHEST)
    inverse = lax.rsqrt(column[:, 0:1] / WIDTH + EPSILON)
    inner = (inverse * column[:, 1:2] - column[:, 2:3]) / TOKENS
    back = inverse * inverse * inverse * inner / WIDTH
    gain_rows = []
    for h in range(HEADS):
        g = gain[h : h + 1]
        normed = raw[h] * inverse
        mismatch = (normed * g - tgt[h]) * (1.0 / TOKENS)
        gain_rows.append(jnp.sum(mismatch * normed, axis=0, keepdims=True))
        res[h] = inverse * (mismatch * g) - raw[h] * back
    lane = iota((16, TOK), 1)
    level_tile = jnp.zeros((16, TOK), F32)
    for h in range(HEADS):
        e = entry[:, h : h + 1]
        d_mix = mm_right_exact(res[h], value, 1, 1)
        d_scores = d_mix * mix[h]
        through = d_mix * sd[h]
        dstate[h] = mm(e * qp[h], res[h], 0, 0)
        d_comb = mm(wk[h], dstate[h], 1, 0)
        dquery[h] = mm(d_scores, kp[h], 1, 0) + e * mm(res[h], ks[h], 1, 1)
        dkey[h] = mm(d_scores, qp[h], 0, 0)
        lines = [
            jnp.sum(jnp.where(level == j, through, 0.0), axis=0, keepdims=True)
            for j in range(LOW + 1)
        ]
        lines += [jnp.sum(ls[j, h] * d_comb, axis=0, keepdims=True) for j in range(CROSS)]
        lines.append(jnp.zeros((16 - LEVELS, TOK), F32))
        summed = jnp.sum(jnp.concatenate(lines, axis=0), axis=1, keepdims=True)
        level_tile = jnp.where(lane == h, summed, level_tile)
    return jnp.concatenate([level_tile] + gain_rows, axis=0)


def at(y, z, k):
    return y * 16 + z * 2 + k


def remote(axis, src, dst, send, recv, target):
    return pltpu.make_async_remote_copy(
        src_ref=src, dst_ref=dst, send_sem=send, recv_sem=recv,
        device_id={axis: target}, device_id_type=MESH,
    )


TWIN, ACROSS, UP, DOWN = range(4)


def whole_kernel(
    q_hbm, k_ref, v_ref, g_ref, wq_hbm, wk_hbm, lw, gain,
    out, levels, gains,
    qs, wq, wk, kv, gates, score, peak, total, tgt, lc, weights, ls, qp, kp, ks, comb, mix, sd, raw, res, local,
    dstate, dquery, dkey, grads, pair, part, from_up, from_down, mine, far,
    sums_box, small_part, small_pair, small_box, small_total, small_far,
    load, send, recv, sums_send, sums_recv, pair_send, pair_recv, ring_send, ring_recv, far_send, far_recv,
    out_send, out_recv, small_send, small_recv,
):
    c = lax.axis_index("seq")
    y, z, k = c // 16, c // 2 % 8, c % 2
    own_pair = c // 2
    targets = (at(y, z, 1 - k), at(1 - y, z, k), at(y, (z + 1) % 8, k), at(y, (z + 7) % 8, k))
    twin, across, up, down = targets
    z_peers = [at(y, (z + d) % 8, k) for d in range(1, 8)]
    me = lax.axis_index("head")
    head_peers = [(me + d) % HEADS for d in range(1, HEADS)]

    loads = [
        pltpu.make_async_copy(q_hbm.at[:, rows(h)], qs.at[rows(h)], load.at[h])
        for h in range(HEADS)
    ]
    loads.append(pltpu.make_async_copy(wq_hbm, wq, load.at[8]))
    loads.append(pltpu.make_async_copy(wk_hbm, wk, load.at[9]))
    for copy in loads:
        copy.start()
    kv[0, c] = k_ref[...]
    kv[1, c] = v_ref[...]
    gates[c] = g_ref[...]

    @pl.when(k == 0)
    def _():
        kv[0, c + 1] = jnp.zeros((TOK, HD), BF)
        kv[1, c + 1] = jnp.zeros((TOK, HD), BF)

    barrier = pltpu.get_barrier_semaphore()
    for partner in [twin, across] + z_peers:
        pl.semaphore_signal(barrier, inc=1, device_id={"seq": partner}, device_id_type=MESH)
    for partner in head_peers:
        pl.semaphore_signal(barrier, inc=1, device_id={"head": partner}, device_id_type=MESH)
    pl.semaphore_wait(barrier, 16)

    def copies(phase, slot, way):
        refs = ((0, gates.at[slot]), (1, kv.at[0, slot])) if phase == 0 else ((2, kv.at[1, slot]),)
        return [
            remote("seq", ref, ref, send.at[i, way, slot], recv.at[i, slot], targets[way])
            for i, ref in refs
        ]

    def push(phase, slot, way, when):
        @pl.when(when)
        def _():
            for copy in copies(phase, slot, way):
                copy.start()

    def pushed(phase, slot, way, when):
        @pl.when(when)
        def _():
            for copy in copies(phase, slot, way):
                copy.wait_send()

    def arrived(phase, slot, when):
        @pl.when(when)
        def _():
            for copy in copies(phase, slot, TWIN):
                copy.wait_recv()

    second = y == 1

    def first_moves(phase, act):
        own = at(y, z, k)
        act(phase, own, ACROSS, y == 0)
        act(phase, own, UP, z <= 6)
        act(phase, own, DOWN, z <= 2)
        act(phase, own, TWIN, k == 0)

    def across_moves(phase, act, wait):
        slot = at(0, z, k)
        wait(phase, slot, second)
        act(phase, slot, UP, second)
        act(phase, slot, DOWN, second)
        act(phase, slot, TWIN, second)

    def round_moves(phase, r, act, wait):
        zs = (z + 8 - r) % 8
        slot, here = at(y, zs, k), z >= r
        wait(phase, slot, here)
        act(phase, slot, UP, here & (z <= 6) & (r < 4))
        act(phase, slot, TWIN, here)
        slot = at(0, zs, k)
        wait(phase, slot, second)
        act(phase, slot, UP, second & (r < 4))
        act(phase, slot, TWIN, second)
        zs = (z + r) % 8
        slot, here = at(y, zs, k), (zs <= 2) & (r < 4)
        wait(phase, slot, here)
        act(phase, slot, DOWN, here & (r < 3))
        act(phase, slot, TWIN, here & (z > zs))
        slot, here = at(0, zs, k), second & (r < 4)
        wait(phase, slot, here)
        act(phase, slot, DOWN, here & (r < 3))
        act(phase, slot, TWIN, here)

    def no_wait(phase, slot, when):
        pass

    def pairs(phase, r, use):
        def one(kind, carry):
            other = kind % 2
            above = kind // 2
            zs = (z + 8 + r * (2 * above - 1)) % 8
            mine_ok = (other == 0) & (r >= 1) & (zs < z) & ((above == 0) & (z >= r) | (above == 1) & (r < 4) & (zs <= 2))
            other_ok = (other == 1) & second & ((above == 0) | (r >= 1) & (r < 4))
            ys = y * (1 - other)

            @pl.when(mine_ok | other_ok)
            def _():
                for copy in copies(phase, at(ys, zs, 1 - k), TWIN):
                    copy.wait_recv()
                use(ys * 8 + zs)

            return carry

        lax.fori_loop(0, 4, one, 0)

    first_moves(0, push)
    first_moves(1, push)
    for copy in loads:
        copy.wait()
    across_moves(0, push, arrived)
    arrived(0, at(y, z, 0), k == 1)
    scored(c, own_pair, True, qs, kv, peak, score)

    def key_round(r, carry):
        @pl.when(r <= 4)
        def _():
            round_moves(0, r, push, arrived)

        @pl.when(r == 1)
        def _():
            student_inside(qs, kv, c, g_ref[...], wq, wk, lw, qp, kp, mix, sd)

        pairs(0, r - 1, lambda p: scored(c, p, False, qs, kv, peak, score))
        return carry

    lax.fori_loop(1, 6, key_round, 0)
    across_moves(1, push, arrived)
    level_weights(c, gates, lc, weights)
    for h in range(HEADS):
        peak[rows(h)] = jnp.broadcast_to(
            jnp.max(peak[rows(h)], axis=1, keepdims=True), (TOK, TOK)
        )
    total[...] = jnp.zeros_like(total)
    tgt[...] = jnp.zeros_like(tgt)
    ls[...] = jnp.zeros_like(ls)
    arrived(1, at(y, z, 0), k == 1)

    @pl.when(k == 1)
    def _():
        keys = kv[0, c - 1].astype(F32).T
        for h in range(HEADS):
            ls[0, h] = mm_right_exact(keys * weights[c - 1, h : h + 1], kv[1, c - 1], 1, 0)

    for h in range(HEADS):
        weighed(own_pair, h, pair_of(kv, 1, own_pair), score, peak, total, tgt)
        local[h] = mm_right_exact(sd[h] * mix_ratio(lw, h), kv[1, c], 1, 0)

    def use_values(p):
        values = pair_of(kv, 1, p)
        keys = pair_of(kv, 0, p).astype(F32).T
        weight = jnp.concatenate([weights[2 * p], weights[2 * p + 1]], axis=1)
        j = jnp.int32(0)
        for b in range(4):
            j = j + (own_pair // (1 << b) != p // (1 << b)).astype(jnp.int32)
        for h in range(HEADS):
            weighed(p, h, values, score, peak, total, tgt)
            ls[j, h] += mm_right_exact(keys * weight[h : h + 1], values, 1, 0)

    def value_round(r, carry):
        @pl.when(r <= 4)
        def _():
            round_moves(1, r, push, arrived)

        pairs(1, r - 1, use_values)
        return carry

    lax.fori_loop(1, 6, value_round, 0)
    for h in range(HEADS):
        tgt[h] = tgt[h] / jnp.sum(total[rows(h)], axis=1, keepdims=True)
    entry = jnp.exp(column_cumulative(g_ref[...]))
    sums_box[me] = student_whole(entry, kv, c, wk, lw, gain, ls, tgt, qp, ks, comb, raw, local)

    outgoing = [
        remote("head", sums_box.at[me], sums_box.at[me], sums_send.at[d], sums_recv.at[me], peer)
        for d, peer in enumerate(head_peers)
    ]
    for copy in outgoing:
        copy.start()
    for d, peer in enumerate(head_peers):
        remote(
            "head", sums_box.at[peer], sums_box.at[peer], sums_send.at[d], sums_recv.at[peer], peer
        ).wait_recv()
    all_sums = sums_box[0]
    for i in range(1, HEADS):
        all_sums = all_sums + sums_box[i]
    small_part[...] = backward_inside(
        all_sums, entry, kv, c, wk, gain, ls, tgt, qp, kp, ks, comb, mix, sd, raw, res, dstate, dquery, dkey
    )

    small_twin = remote("seq", small_part, small_pair, small_send.at[0], small_recv.at[8], twin)
    small_twin.start()
    key = kv[0, c]
    order = [(z + d) % 8 for d in (4, 3, 5, 2, 6, 1, 7, 0)]

    def to_twin(h):
        return remote("seq", grads.at[1 - k, h], pair.at[h], pair_send.at[h], pair_recv.at[h], twin)

    for h in order:
        q_rows = qs[pl.ds(pl.multiple_of(h * TOK, TOK), TOK)]
        grads[0, h] = mm_left_exact(q_rows, dquery[h], 0, 0)
        grads[1, h] = mm(comb[h], dstate[h], 1, 1) + mm_left_exact(key, dkey[h], 0, 0)
        to_twin(h).start()
    small_twin.wait_recv()
    small_box[z] = small_part[...] + small_pair[...]
    small_out = [
        remote("seq", small_box.at[z], small_box.at[z], small_send.at[d], small_recv.at[z], peer)
        for d, peer in enumerate(z_peers, 1)
    ]
    for copy in small_out:
        copy.start()

    def half(a):
        return pl.ds(a * HALF, HALF)

    def hop(way, i, h, a):
        box = from_up if way == DOWN else from_down
        return remote(
            "seq", part.at[h, half(a)], box.at[i, half(a)], ring_send.at[way - 2, i, a],
            ring_recv.at[way - 2, i, a], targets[way],
        )

    def summed(way, i, h):
        to_twin(h).wait_recv()
        for a in range(2):
            held = grads[k, h, half(a)] + pair[h, half(a)]
            if i:
                hop(way, i - 1, h, a).wait_recv()
                held = held + (from_up if way == DOWN else from_down)[i - 1, half(a)]
            part[h, half(a)] = held
            hop(way, i, h, a).start()

    hops = []
    for i in range(4):
        summed(DOWN, i, (z + 4 + i) % 8)
        hops.append((DOWN, i, (z + 4 + i) % 8))
        if i < 3:
            summed(UP, i, (z + 3 - i) % 8)
            hops.append((UP, i, (z + 3 - i) % 8))
    to_twin(z).wait_recv()

    def swap(a):
        return remote(
            "seq", mine.at[half(a)], far.at[half(a)], far_send.at[a], far_recv.at[a], across
        )

    for a in range(2):
        hop(UP, 2, z, a).wait_recv()
        held = grads[k, z, half(a)] + pair[z, half(a)] + from_down[2, half(a)]
        hop(DOWN, 3, z, a).wait_recv()
        mine[half(a)] = held + from_up[3, half(a)]
        swap(a).start()
    for d, h in enumerate([(z + d) % 8 for d in range(1, 8)], 1):
        remote(
            "seq", small_box.at[h], small_box.at[h], small_send.at[d], small_recv.at[h], z_peers[d - 1]
        ).wait_recv()
    held = small_box[0]
    for i in range(1, 8):
        held = held + small_box[i]
    small_total[...] = held
    small_swap = remote("seq", small_total, small_far, small_send.at[8], small_recv.at[9], across)
    small_swap.start()

    def spread(way, h, a):
        ref = out.at[k, h, half(a)]
        return remote("seq", ref, ref, out_send.at[way, h, a], out_recv.at[0, h, a], targets[way])

    def to_out_twin(h, a):
        ref = out.at[k, h, half(a)]
        return remote("seq", ref, ref, out_send.at[0, h, a], out_recv.at[1, h, a], twin)

    pending = []

    def go(copy):
        copy.start()
        pending.append(copy)

    for a in range(2):
        swap(a).wait_recv()
        out[k, z, half(a)] = mine[half(a)] + far[half(a)]
        go(spread(UP, z, a))
        go(spread(DOWN, z, a))
        go(to_out_twin(z, a))
    small_swap.wait_recv()
    final = small_total[...] + small_far[...]
    tile = jnp.concatenate([final[:16], jnp.zeros((TOK - 16, TOK), F32)], axis=0).T
    levels[...] = tile[:HEADS, :LEVELS]
    gains[...] = final[16:]
    for r in range(1, 5):
        for a in range(2):
            h = (z + 8 - r) % 8
            spread(UP, h, a).wait_recv()
            if r < 4:
                go(spread(UP, h, a))
            go(to_out_twin(h, a))
            if r < 4:
                h = (z + r) % 8
                spread(DOWN, h, a).wait_recv()
                if r < 3:
                    go(spread(DOWN, h, a))
                go(to_out_twin(h, a))
    for h in range(8):
        for a in range(2):
            ref = out.at[1 - k, h, half(a)]
            remote("seq", ref, ref, out_send.at[0, h, a], out_recv.at[1, h, a], twin).wait_recv()

    for phase in range(2):
        first_moves(phase, pushed)
        across_moves(phase, pushed, no_wait)

        def sent(r, carry, phase=phase):
            round_moves(phase, r, pushed, no_wait)
            return carry

        lax.fori_loop(1, 5, sent, 0)
    for copy in outgoing + [small_twin] + small_out + [small_swap] + pending:
        copy.wait_send()
    for h in order:
        to_twin(h).wait_send()
    for way, i, h in hops:
        for a in range(2):
            hop(way, i, h, a).wait_send()
    for a in range(2):
        swap(a).wait_send()


def mix_ratio(lw, h):
    level = local_levels()
    mask = jnp.full((TOK, TOK), lw[h, 0], F32)
    for j in range(1, LOW + 1):
        mask = jnp.where(level == j, lw[h, j], mask)
    return mask


VM = pl.BlockSpec(memory_space=pltpu.VMEM)
SM = pl.BlockSpec(memory_space=pltpu.SMEM)
ANY = pl.BlockSpec(memory_space=pl.ANY)
DMA = pltpu.SemaphoreType.DMA


def shaped(shape, dtype=F32):
    return jax.ShapeDtypeStruct(shape, dtype)


def on_device(queries, key_vectors, value_vectors, log_gate, query_map, key_map, lw, norm_gain):
    matrix = pltpu.VMEM((HEADS, TOK, HD), F32)
    small = pltpu.VMEM((SMALL, TOK), F32)
    one = pltpu.VMEM((TOK, HD), F32)
    out, levels, gains = pl.pallas_call(
        whole_kernel,
        out_shape=(shaped((2, HEADS, HD, HD)), shaped((HEADS, LEVELS)), shaped((HEADS, HD))),
        in_specs=[ANY, VM, VM, VM, ANY, ANY, SM, VM],
        out_specs=(VM,) * 3,
        scratch_shapes=[
            pltpu.VMEM((HEADS * TOK, HD), BF),
            matrix,
            matrix,
            pltpu.VMEM((2, SPANS, TOK, HD), BF),
            pltpu.VMEM((SPANS, HEADS, TOK), F32),
            pltpu.VMEM((SPANS // 2, HEADS * TOK, 2 * TOK), F32),
            pltpu.VMEM((HEADS * TOK, TOK), F32),
            pltpu.VMEM((HEADS * TOK, TOK), F32),
            matrix,
            pltpu.VMEM((SPANS * HEADS, TOK), F32),
            pltpu.VMEM((SPANS, HEADS, TOK), F32),
            pltpu.VMEM((CROSS, HEADS, HD, HD), F32),
            *[matrix] * 12,
            pltpu.VMEM((2, HEADS, HD, HD), F32),
            matrix,
            matrix,
            pltpu.VMEM((4, HD, HD), F32),
            pltpu.VMEM((3, HD, HD), F32),
            one,
            one,
            pltpu.VMEM((HEADS, 8, TOK), F32),
            small,
            small,
            pltpu.VMEM((8, SMALL, TOK), F32),
            small,
            small,
            DMA((10,)),
            DMA((3, 4, SPANS)),
            DMA((3, SPANS)),
            DMA((7,)),
            DMA((HEADS,)),
            DMA((8,)),
            DMA((8,)),
            DMA((2, 4, 2)),
            DMA((2, 4, 2)),
            DMA((2,)),
            DMA((2,)),
            DMA((4, 8, 2)),
            DMA((2, 8, 2)),
            DMA((9,)),
            DMA((10,)),
        ],
        compiler_params=pltpu.CompilerParams(
            collective_id=0, has_side_effects=True, vmem_limit_bytes=LIMIT
        ),
        name="distill",
    )(
        queries, key_vectors, value_vectors, log_gate, query_map, key_map, lw,
        norm_gain.reshape(HEADS, HD),
    )
    return out[0], out[1], levels, gains.reshape(-1)


def solution(mesh):
    return jax.shard_map(
        on_device,
        mesh=mesh,
        in_specs=(
            P("seq", "head"),
            P("seq", "head"),
            P("seq", "head"),
            P("head", "seq"),
            P("head", None, None),
            P("head", None, None),
            P("head", None),
            P("head"),
        ),
        out_specs=(P("head", None, None), P("head", None, None), P("head", None), P("head")),
        check_vma=False,
    )
```

profile of v0, /device:TPU:1, one launch (start us, length us, event | category | flops | bytes accessed | tf_op | source)
XLA Modules:
  0.0 100.5 jit_solution(6670528346151507533)
XLA Ops:
  0.6 96.3 %distill.1 = (f32[2,8,128,128]{3,2,1,0:T(8,128)}, f32[8,13]{1,0:T(8,128)}, f32[8,128]{1,0:T(8,128)}) custom-call(bf16[128,1024]{1,0:T(8,128)(2,1)} %q_hbm.1, bf16[128,128]{1,0:T(8,128)(2,1)} %k_ref.1, bf16[128,128]{1,0:T(8,128)(2,1)} %v_ref.1, f32[8,128]{1,0:T(8,128)} %g_ref.1, f32[8,128,128]{2,1,0:T(8,128)} %wq_hbm.1, f32[8,128,128]{2,1,0:T(8,128)} %wk_hbm.1, ...), custom_call_target="tpu_custom_call" | custom-call | tf_op jit(solution)/shard_map/distill/pallas_call | solution.py:586
  97.0 0.0 copy-start.1
  97.0 2.3 %slice_bitcast_fusion = (f32[8,128,128]{2,1,0:T(8,128)}, f32[8,128,128]{2,1,0:T(8,128)}) fusion(f32[2,8,128,128]{3,2,1,0:T(8,128)} %get-tuple-element.7), kind=kLoop, calls=%fused_computation | loop fusion | bytes 2097152 | tf_op jit(solution)/shard_map/squeeze | solution.py:642
  99.2 0.0 copy-done.1
  99.2 0.0 copy-start
  99.2 0.6 copy.14
  99.8 0.1 copy-done
  99.9 0.6 copy.15
Async XLA Ops:
  97.0 2.3 %copy-start.1 = (f32[8,13]{1,0:T(8,128)S(1)}, f32[8,13]{1,0:T(8,128)}, u32[]{:S(2)}) copy-start(f32[8,13]{1,0:T(8,128)} %get-tuple-element.18) | copy-start | bytes 1252
  99.2 0.7 copy-start
where the time goes:
time: 101 us
  Pallas kernels  96.3 us (95%)
  local copies, waits for them, and re-layouts  3.55 us (4%)
    pallas_call x1, Pallas kernels, on_device(): pl.pallas_call(whole_kernel, out_shape=(shaped((2, HEADS, HD, HD)), shape...  96.3 us
    squeeze x1, local copies, waits for them, and re-layouts, on_device(): return (out[0], out[1], levels, gains.reshape(-1))  2.27 us

commit v1 on v0

v1 whole, which is shorter than its diff:
```python
import jax
import jax.numpy as jnp
from jax import lax
from jax.experimental import pallas as pl
from jax.experimental.pallas import tpu as pltpu
from jax.sharding import PartitionSpec as P

F32 = jnp.float32
BF = jnp.bfloat16
HIGHEST = lax.Precision.HIGHEST
MESH = pl.DeviceIdType.MESH
NEGATIVE = -1e30
EPSILON = 1e-05
HD = 128
TOK = 128
HEADS = 8
SPANS = 32
LEVELS = 13
LOW = 7
CROSS = 5
TOKENS = TOK * SPANS
WIDTH = 64 * HD
SMALL = 24
GATE_ROWS = 32
VALUE_ROWS = 128 + GATE_ROWS
PIECE = 64 + 8
HALF = HD // 2
LOG2E = 1.4426950408889634
SCALE = HD**-0.5 * LOG2E
LIMIT = 58 << 20


def pieces(a):
    high = a.astype(BF)
    return high, (a - high.astype(F32)).astype(BF)


def dg(a, b, ca, cb, precision=None):
    return lax.dot_general(
        a, b, (((ca,), (cb,)), ((), ())), preferred_element_type=F32, precision=precision
    )


def halves(o):
    n = o.shape[1] // 2
    return o[:, :n] + o[:, n:]


def mm(a, b, ca, cb):
    bh, bl = pieces(b)
    left = jnp.concatenate(pieces(a), axis=ca)
    right = jnp.concatenate(
        [jnp.concatenate([bh, bh], axis=cb), jnp.concatenate([bl, bl], axis=cb)], axis=1 - cb
    )
    return halves(dg(left, right, ca, cb))


def mm_left_exact(a, b, ca, cb):
    return halves(dg(a, jnp.concatenate(pieces(b), axis=1 - cb), ca, cb))


def mm_right_exact(a, b, ca, cb):
    return dg(jnp.concatenate(pieces(a), axis=ca), jnp.concatenate([b, b], axis=cb), ca, cb)


def iota(shape, dim):
    return lax.broadcasted_iota(jnp.int32, shape, dim)


def local_levels():
    x = jnp.bitwise_xor(iota((TOK, TOK), 0), iota((TOK, TOK), 1))
    level = jnp.zeros_like(x)
    for bit in range(LOW):
        level = level + (x >= 1 << bit).astype(jnp.int32)
    return level


def rows(h):
    return slice(h * TOK, (h + 1) * TOK)


def column_cumulative(gates):
    lower = (iota((TOK, TOK), 1) <= iota((TOK, TOK), 0)).astype(F32)
    return dg(lower, gates, 1, 1, HIGHEST)


def pair_of(ref, p):
    return jnp.concatenate([ref[2 * p, :TOK], ref[2 * p + 1, :TOK]], axis=0)


def scored(c, p, masked, qs, keys_all, peak, score):
    keys = pair_of(keys_all, p)
    for h in range(HEADS):
        s = dg(qs[rows(h)], keys, 1, 1)
        if masked:
            place_of = 2 * TOK * p + iota((TOK, 2 * TOK), 1)
            s = jnp.where(place_of <= c * TOK + iota((TOK, 2 * TOK), 0), s, NEGATIVE)
        score[p, rows(h)] = s
        top = jnp.maximum(s[:, :TOK], s[:, TOK:])
        peak[rows(h)] = top if masked else jnp.maximum(peak[rows(h)], top)


def weighed(p, h, values, score, peak, total, tgt):
    s = score[p, rows(h)]
    top = peak[rows(h)]
    w0 = jnp.exp2((s[:, :TOK] - top) * SCALE)
    w1 = jnp.exp2((s[:, TOK:] - top) * SCALE)
    total[rows(h)] += w0 + w1
    tgt[h] += dg(jnp.concatenate([w0.astype(BF), w1.astype(BF)], axis=1), values, 1, 0)


def level_weights(c, vals, lc, weights):
    upper = (iota((TOK, TOK), 0) <= iota((TOK, TOK), 1)).astype(BF)
    lc[...] = dg(vals[:, TOK:].reshape(SPANS * GATE_ROWS, TOK), upper, 1, 0)

    def step(i, since):
        x = c - 1 - i
        three = lc[pl.ds(pl.multiple_of(x * GATE_ROWS, GATE_ROWS), 3 * HEADS)]
        own = three[:HEADS] + three[HEADS : 2 * HEADS] + three[2 * HEADS :]
        since = since + own[:, TOK - 1 :]
        weights[x] = jnp.exp(since - own)
        return since

    lax.fori_loop(0, c, step, jnp.zeros((HEADS, 1), F32))


def gate_pieces(gate):
    high = gate.astype(BF).astype(F32)
    middle = (gate - high).astype(BF).astype(F32)
    low = gate - high - middle
    return jnp.concatenate([high, middle, low, jnp.zeros_like(gate)], axis=0).astype(BF)


def student_inside(qs, key, gate, wq, wk, lw, qp, kp, mix, sd):
    upper = (iota((TOK, TOK), 0) <= iota((TOK, TOK), 1)).astype(F32)
    row_cum = dg(gate, upper, 1, 0, HIGHEST)
    col_cum = column_cumulative(gate)
    causal = iota((TOK, TOK), 1) <= iota((TOK, TOK), 0)
    level = local_levels()
    for h in range(HEADS):
        qp[h] = mm_left_exact(qs[rows(h)], wq[h], 1, 0)
        kp[h] = mm_left_exact(key, wk[h], 1, 0)
    for h in range(HEADS):
        decay = jnp.exp(
            jnp.where(causal, col_cum[:, h : h + 1] - row_cum[h : h + 1], NEGATIVE)
        )
        mask = jnp.full((TOK, TOK), lw[h, 0], F32)
        for j in range(1, LOW + 1):
            mask = jnp.where(level == j, lw[h, j], mask)
        sd[h] = mm(qp[h], kp[h], 1, 1) * decay
        mix[h] = decay * mask


def student_whole(entry, wk, lw, gain, ls, tgt, qp, ks, comb, raw, local):
    for h in range(HEADS):
        combined = lw[h, LOW + 1] * ls[0, h]
        for j in range(1, CROSS):
            combined = combined + lw[h, LOW + 1 + j] * ls[j, h]
        comb[h] = combined
        ks[h] = mm(wk[h], combined, 0, 0)
    square = jnp.zeros((TOK, HD), F32)
    scaled = jnp.zeros((TOK, HD), F32)
    against = jnp.zeros((TOK, HD), F32)
    for h in range(HEADS):
        r = local[h] + entry[:, h : h + 1] * mm(qp[h], ks[h], 1, 0)
        raw[h] = r
        rg = r * gain[h : h + 1]
        square = square + r * r
        scaled = scaled + rg * rg
        against = against + tgt[h] * rg
    one = jnp.ones((8, HD), F32)
    tile = [dg(one, x, 1, 1, HIGHEST) for x in (square, scaled, against)]
    return jnp.concatenate([t[:1] for t in tile] + [tile[0][:5]], axis=0)


def backward_inside(
    all_sums, entry, value, wk, gain, ls, tgt, qp, kp, ks, mix, sd, raw, res, dstate, dquery, dkey
):
    eye = (iota((TOK, TOK), 0) == iota((TOK, TOK), 1)).astype(F32)
    level = local_levels()
    column = dg(eye, all_sums, 1, 1, HIGHEST)
    inverse = lax.rsqrt(column[:, 0:1] / WIDTH + EPSILON)
    inner = (inverse * column[:, 1:2] - column[:, 2:3]) / TOKENS
    back = inverse * inverse * inverse * inner / WIDTH
    gain_rows = []
    for h in range(HEADS):
        g = gain[h : h + 1]
        normed = raw[h] * inverse
        mismatch = (normed * g - tgt[h]) * (1.0 / TOKENS)
        gain_rows.append(jnp.sum(mismatch * normed, axis=0, keepdims=True))
        res[h] = inverse * (mismatch * g) - raw[h] * back
    lane = iota((16, TOK), 1)
    level_tile = jnp.zeros((16, TOK), F32)
    for h in range(HEADS):
        e = entry[:, h : h + 1]
        d_mix = mm_right_exact(res[h], value, 1, 1)
        d_scores = d_mix * mix[h]
        through = d_mix * sd[h]
        dstate[h] = mm(e * qp[h], res[h], 0, 0)
        d_comb = mm(wk[h], dstate[h], 1, 0)
        dquery[h] = mm(d_scores, kp[h], 1, 0) + e * mm(res[h], ks[h], 1, 1)
        dkey[h] = mm(d_scores, qp[h], 0, 0)
        lines = [
            jnp.sum(jnp.where(level == j, through, 0.0), axis=0, keepdims=True)
            for j in range(LOW + 1)
        ]
        lines += [jnp.sum(ls[j, h] * d_comb, axis=0, keepdims=True) for j in range(CROSS)]
        lines.append(jnp.zeros((16 - LEVELS, TOK), F32))
        summed = jnp.sum(jnp.concatenate(lines, axis=0), axis=1, keepdims=True)
        level_tile = jnp.where(lane == h, summed, level_tile)
    return jnp.concatenate([level_tile] + gain_rows, axis=0)


def at(y, z, k):
    return y * 16 + z * 2 + k


def remote(axis, src, dst, send, recv, target):
    return pltpu.make_async_remote_copy(
        src_ref=src, dst_ref=dst, send_sem=send, recv_sem=recv,
        device_id={axis: target}, device_id_type=MESH,
    )


def whole_kernel(
    q_hbm, k_ref, v_ref, g_ref, wq_hbm, wk_hbm, lw, gain,
    out, levels, gains,
    qs, wq, wk, keys_all, vals, score, peak, total, tgt, lc, weights, ls, qp, kp, ks, comb, mix, sd, raw, res, local,
    dstate, dquery, dkey, grads, pair, part, box, done, sums_box, small_part, small_pair, small_sum,
    load, own_send, relay_send, twin_send, recv, sums_send, sums_recv, pair_send, pair_recv,
    part_send, part_recv, done_send, done_recv, small_sem,
):
    c = lax.axis_index("seq")
    y, z, k = c // 16, c // 2 % 8, c % 2
    own_pair = c // 2
    second = y == 1
    twin, across = at(y, z, 1 - k), at(1 - y, z, k)
    far_first = (4, 3, 5, 2, 6, 1, 7)
    me = lax.axis_index("head")
    head_peers = [(me + d) % HEADS for d in range(1, HEADS)]

    barrier = pltpu.get_barrier_semaphore()
    for d in range(8):
        for other in range(2):
            if d or other:
                target = at((y + other) % 2, (z + d) % 8, k)
                pl.semaphore_signal(barrier, inc=1, device_id={"seq": target}, device_id_type=MESH)
    pl.semaphore_signal(barrier, inc=1, device_id={"seq": twin}, device_id_type=MESH)
    for peer in head_peers:
        pl.semaphore_signal(barrier, inc=1, device_id={"head": peer}, device_id_type=MESH)

    loads = [
        pltpu.make_async_copy(q_hbm.at[:, rows(h)], qs.at[rows(h)], load.at[h])
        for h in range(HEADS)
    ]
    loads.append(pltpu.make_async_copy(wq_hbm, wq, load.at[8]))
    loads.append(pltpu.make_async_copy(wk_hbm, wk, load.at[9]))
    for copy in loads:
        copy.start()
    keys_all[c] = k_ref[...]
    vals[c, :TOK] = v_ref[...]
    vals[c, TOK:] = gate_pieces(g_ref[...])

    @pl.when(k == 0)
    def _():
        keys_all[c + 1] = jnp.zeros((TOK, HD), BF)
        vals[c + 1] = jnp.zeros((VALUE_ROWS, HD), BF)

    for copy in loads:
        copy.wait()
    pl.semaphore_wait(barrier, 23)

    def block(phase, slot):
        return keys_all.at[slot] if phase == 0 else vals.at[slot]

    def copy_of(phase, slot, sem, target):
        ref = block(phase, slot)
        return remote("seq", ref, ref, sem, recv.at[phase, slot], target)

    def to_twin(phase, slot):
        return copy_of(phase, slot, twin_send.at[phase, slot], twin)

    def to_across(phase):
        return copy_of(phase, c, own_send.at[phase, 0], across)

    def to_row(phase, d):
        return copy_of(phase, c, own_send.at[phase, d], at(y, (z + d) % 8, k))

    def relayed(phase, d):
        return copy_of(phase, at(0, z, k), relay_send.at[phase, d], at(y, (z + d) % 8, k))

    def act(when, copy, wait=False):
        @pl.when(when)
        def _():
            if wait:
                copy.wait_send()
            else:
                copy.start()

    def own_moves(phase, wait=False):
        act(y == 0, to_across(phase), wait)
        act(k == 0, to_twin(phase, c), wait)
        for d in far_first:
            act(z + d < 8, to_row(phase, d), wait)

    def arrived(phase, slot):
        to_twin(phase, slot).wait_recv()

    def relay(phase):
        @pl.when(second)
        def _():
            slot = at(0, z, k)
            arrived(phase, slot)
            for d in far_first:
                relayed(phase, d).start()
            to_twin(phase, slot).start()

    def chip_of(i):
        d = jnp.where(i % 2 == 1, (i + 1) // 2, 8 - i // 2)
        return (z + 8 - d) % 8

    def forward(phase, i):
        zs = chip_of(i)

        @pl.when(zs < z)
        def _():
            slot = at(y, zs, k)
            arrived(phase, slot)
            to_twin(phase, slot).start()

        @pl.when(second)
        def _():
            slot = at(0, zs, k)
            arrived(phase, slot)
            to_twin(phase, slot).start()

    def pairs(phase, i, use):
        zs = jnp.where(i == 0, z, chip_of(i))

        def one(other, carry):
            @pl.when((other == 0) & (zs < z) | (other == 1) & second)
            def _():
                ys = y * (1 - other)
                arrived(phase, at(ys, zs, 1 - k))
                use(ys * 8 + zs)

            return carry

        lax.fori_loop(0, 2, one, 0)

    own_moves(0)
    own_moves(1)
    student_inside(qs, k_ref[...], g_ref[...], wq, wk, lw, qp, kp, mix, sd)
    relay(0)
    relay(1)

    @pl.when(k == 1)
    def _():
        arrived(0, c - 1)

    scored(c, own_pair, True, qs, keys_all, peak, score)

    def key_step(i, carry):
        @pl.when(i < 8)
        def _():
            forward(0, i)

        pairs(0, i - 1, lambda p: scored(c, p, False, qs, keys_all, peak, score))
        return carry

    lax.fori_loop(1, 9, key_step, 0)

    def value_forward(i, carry):
        forward(1, i)
        return carry

    lax.fori_loop(1, 8, value_forward, 0)
    for h in range(HEADS):
        peak[rows(h)] = jnp.broadcast_to(
            jnp.max(peak[rows(h)], axis=1, keepdims=True), (TOK, TOK)
        )
    total[...] = jnp.zeros_like(total)
    tgt[...] = jnp.zeros_like(tgt)
    ls[...] = jnp.zeros_like(ls)

    @pl.when(k == 1)
    def _():
        arrived(1, c - 1)

    level = local_levels()
    for h in range(HEADS):
        weighed(own_pair, h, pair_of(vals, own_pair), score, peak, total, tgt)
        mask = jnp.full((TOK, TOK), lw[h, 0], F32)
        for j in range(1, LOW + 1):
            mask = jnp.where(level == j, lw[h, j], mask)
        local[h] = mm_right_exact(sd[h] * mask, v_ref[...], 1, 0)

    def all_here(i, carry):
        zs = jnp.where(i == 0, z, chip_of(i))

        @pl.when(zs < z)
        def _():
            arrived(1, at(y, zs, 1 - k))

        @pl.when(second)
        def _():
            arrived(1, at(0, zs, 1 - k))

        return carry

    lax.fori_loop(0, 8, all_here, 0)
    level_weights(c, vals, lc, weights)

    @pl.when(k == 1)
    def _():
        keys = keys_all[c - 1].astype(F32).T
        for h in range(HEADS):
            ls[0, h] = mm_right_exact(keys * weights[c - 1, h : h + 1], vals[c - 1, :TOK], 1, 0)

    def use_values(p, carry):
        values = pair_of(vals, p)
        keys = pair_of(keys_all, p).astype(F32).T
        weight = jnp.concatenate([weights[2 * p], weights[2 * p + 1]], axis=1)
        j = jnp.int32(0)
        for b in range(4):
            j = j + (own_pair // (1 << b) != p // (1 << b)).astype(jnp.int32)
        for h in range(HEADS):
            weighed(p, h, values, score, peak, total, tgt)
            ls[j, h] += mm_right_exact(keys * weight[h : h + 1], values, 1, 0)
        return carry

    lax.fori_loop(0, own_pair, use_values, 0)
    for h in range(HEADS):
        tgt[h] = tgt[h] / jnp.sum(total[rows(h)], axis=1, keepdims=True)
    entry = jnp.exp(column_cumulative(g_ref[...]))
    sums_box[me] = student_whole(entry, wk, lw, gain, ls, tgt, qp, ks, comb, raw, local)

    outgoing = [
        remote("head", sums_box.at[me], sums_box.at[me], sums_send.at[d], sums_recv.at[me], peer)
        for d, peer in enumerate(head_peers)
    ]
    for copy in outgoing:
        copy.start()
    for d, peer in enumerate(head_peers):
        remote(
            "head", sums_box.at[peer], sums_box.at[peer], sums_send.at[d], sums_recv.at[peer], peer
        ).wait_recv()
    all_sums = sums_box[0]
    for i in range(1, HEADS):
        all_sums = all_sums + sums_box[i]
    small_part[...] = backward_inside(
        all_sums, entry, v_ref[...], wk, gain, ls, tgt, qp, kp, ks, mix, sd, raw, res, dstate, dquery, dkey
    )

    small_twin = remote("seq", small_part, small_pair, small_sem.at[0], small_sem.at[1], twin)
    small_twin.start()
    order = [(z + d) % 8 for d in far_first + (0,)]

    def twin_part(h):
        return remote("seq", grads.at[1 - k, h], pair.at[h], pair_send.at[h], pair_recv.at[h], twin)

    for h in order:
        q_rows = qs[pl.ds(pl.multiple_of(h * TOK, TOK), TOK)]
        grads[0, h] = mm_left_exact(q_rows, dquery[h], 0, 0)
        grads[1, h] = mm(comb[h], dstate[h], 1, 1) + mm_left_exact(k_ref[...], dkey[h], 0, 0)
        twin_part(h).start()
    small_twin.wait_recv()
    small_sum[...] = small_part[...] + small_pair[...]
    here = y * 8 + z

    def piece_to(h, a):
        return remote(
            "seq", part.at[h, a], box.at[here], part_send.at[h, a], part_recv.at[here], at(a, h, k)
        )

    for h in order:
        twin_part(h).wait_recv()
        tile = h % 3
        for a in range(2):
            part[h, a, :HALF] = grads[k, h, a * HALF : (a + 1) * HALF] + pair[h, a * HALF : (a + 1) * HALF]
            part[h, a, HALF:] = small_sum[pl.ds(pl.multiple_of(tile * 8, 8), 8)]
            act((h != z) | (a != y), piece_to(h, a))
    box[here] = part[z, y]
    for h in order:
        for a in range(2):
            source = a * 8 + h

            @pl.when((h != z) | (a != y))
            def _(source=source, h=h, a=a):
                remote(
                    "seq", part.at[h, a], box.at[source], part_send.at[h, a], part_recv.at[source], at(a, h, k)
                ).wait_recv()

    whole = box[0]
    for i in range(1, 16):
        whole = whole + box[i]
    done[k, z, y] = whole

    def sum_to(h, a):
        ref = done.at[k, z, y]
        return remote("seq", ref, ref, done_send.at[0, h, a], done_recv.at[0, z, y], at(a, h, k))

    def sum_from(h, a):
        ref = done.at[k, h, a]
        return remote("seq", ref, ref, done_send.at[0, h, a], done_recv.at[0, h, a], at(a, h, k))

    def sum_twin(core, h, a):
        ref = done.at[core, h, a]
        return remote("seq", ref, ref, done_send.at[1, h, a], done_recv.at[1, h, a], twin)

    for h in order:
        for a in range(2):
            act((h != z) | (a != y), sum_to(h, a))
    sum_twin(k, z, y).start()
    for h in [(z + d) % 8 for d in (0, 1, 7, 2, 6, 3, 5, 4)]:
        for a in range(2):

            @pl.when((h != z) | (a != y))
            def _(h=h, a=a):
                sum_from(h, a).wait_recv()
                sum_twin(k, h, a).start()

    for a in range(2):
        out[k, :, a * HALF : (a + 1) * HALF] = done[k, :, a, :HALF]
    tile = jnp.concatenate(
        [done[k, t, 0, HALF:] for t in range(2)] + [jnp.zeros((TOK - 16, TOK), F32)], axis=0
    ).T
    levels[...] = tile[:HEADS, :LEVELS]
    gains[...] = done[k, 2, 0, HALF:]
    for h in range(8):
        for a in range(2):
            sum_twin(1 - k, h, a).wait_recv()
    for a in range(2):
        out[1 - k, :, a * HALF : (a + 1) * HALF] = done[1 - k, :, a, :HALF]

    for phase in range(2):
        own_moves(phase, True)

        @pl.when(second)
        def _(phase=phase):
            for d in far_first:
                relayed(phase, d).wait_send()
            to_twin(phase, at(0, z, k)).wait_send()

        def sent(i, carry, phase=phase):
            zs = chip_of(i)
            act(zs < z, to_twin(phase, at(y, zs, k)), True)
            act(second, to_twin(phase, at(0, zs, k)), True)
            return carry

        lax.fori_loop(1, 8, sent, 0)
    for copy in outgoing + [small_twin]:
        copy.wait_send()
    for h in order:
        twin_part(h).wait_send()
        for a in range(2):
            act((h != z) | (a != y), piece_to(h, a), True)
            act((h != z) | (a != y), sum_to(h, a), True)
            sum_twin(k, h, a).wait_send()


VM = pl.BlockSpec(memory_space=pltpu.VMEM)
SM = pl.BlockSpec(memory_space=pltpu.SMEM)
ANY = pl.BlockSpec(memory_space=pl.ANY)
DMA = pltpu.SemaphoreType.DMA


def shaped(shape, dtype=F32):
    return jax.ShapeDtypeStruct(shape, dtype)


def on_device(queries, key_vectors, value_vectors, log_gate, query_map, key_map, lw, norm_gain):
    matrix = pltpu.VMEM((HEADS, TOK, HD), F32)
    small = pltpu.VMEM((SMALL, TOK), F32)
    out, levels, gains = pl.pallas_call(
        whole_kernel,
        out_shape=(shaped((2, HEADS, HD, HD)), shaped((HEADS, LEVELS)), shaped((HEADS, HD))),
        in_specs=[ANY, VM, VM, VM, ANY, ANY, SM, VM],
        out_specs=(VM,) * 3,
        scratch_shapes=[
            pltpu.VMEM((HEADS * TOK, HD), BF),
            matrix,
            matrix,
            pltpu.VMEM((SPANS, TOK, HD), BF),
            pltpu.VMEM((SPANS, VALUE_ROWS, HD), BF),
            pltpu.VMEM((SPANS // 2, HEADS * TOK, 2 * TOK), F32),
            pltpu.VMEM((HEADS * TOK, TOK), F32),
            pltpu.VMEM((HEADS * TOK, TOK), F32),
            matrix,
            pltpu.VMEM((SPANS * GATE_ROWS, TOK), F32),
            pltpu.VMEM((SPANS, HEADS, TOK), F32),
            pltpu.VMEM((CROSS, HEADS, HD, HD), F32),
            *[matrix] * 12,
            pltpu.VMEM((2, HEADS, HD, HD), F32),
            matrix,
            pltpu.VMEM((HEADS, 2, PIECE, HD), F32),
            pltpu.VMEM((16, PIECE, HD), F32),
            pltpu.VMEM((2, HEADS, 2, PIECE, HD), F32),
            pltpu.VMEM((HEADS, 8, TOK), F32),
            small,
            small,
            small,
            DMA((10,)),
            DMA((2, 8)),
            DMA((2, 8)),
            DMA((2, SPANS)),
            DMA((2, SPANS)),
            DMA((7,)),
            DMA((HEADS,)),
            DMA((8,)),
            DMA((8,)),
            DMA((8, 2)),
            DMA((16,)),
            DMA((2, 8, 2)),
            DMA((2, 8, 2)),
            DMA((2,)),
        ],
        compiler_params=pltpu.CompilerParams(
            collective_id=0, has_side_effects=True, vmem_limit_bytes=LIMIT
        ),
        name="distill",
    )(
        queries, key_vectors, value_vectors, log_gate, query_map, key_map, lw,
        norm_gain.reshape(HEADS, HD),
    )
    return out[0], out[1], levels, gains.reshape(-1)


def solution(mesh):
    return jax.shard_map(
        on_device,
        mesh=mesh,
        in_specs=(
            P("seq", "head"),
            P("seq", "head"),
            P("seq", "head"),
            P("head", "seq"),
            P("head", None, None),
            P("head", None, None),
            P("head", None),
            P("head"),
        ),
        out_specs=(P("head", None, None), P("head", None, None), P("head", None), P("head")),
        check_vma=False,
    )
```

time: 101 us -> 104 us (1.030)
  Pallas kernels: 96.3 us -> 99.3 us
    pallas_call x1, Pallas kernels: 96.3 us -> 99.3 us  [on_device(): pl.pallas_call(whole_kernel, out_shape=(shaped((2, HEADS, HD, HD)), shape...]
where the time goes in v1:
time: 104 us; the launch traced here: 103 us
  Pallas kernels  99.3 us (95%)
  local copies, waits for them, and re-layouts  3.55 us (3%)
    pallas_call x1, Pallas kernels, on_device(): pl.pallas_call(whole_kernel, out_shape=(shaped((2, HEADS, HD, HD)), shape...  99.3 us
    squeeze x1, local copies, waits for them, and re-layouts, on_device(): return (out[0], out[1], levels, gains.reshape(-1))  2.27 us

profile of v1, /device:TPU:1, one launch (start us, length us, event | category | flops | bytes accessed | tf_op | source)
XLA Modules:
  0.0 103.5 jit_solution(4507157151776344383)
XLA Ops:
  0.6 99.3 %distill.1 = (f32[2,8,128,128]{3,2,1,0:T(8,128)}, f32[8,13]{1,0:T(8,128)}, f32[8,128]{1,0:T(8,128)}) custom-call(bf16[128,1024]{1,0:T(8,128)(2,1)} %q_hbm.1, bf16[128,128]{1,0:T(8,128)(2,1)} %k_ref.1, bf16[128,128]{1,0:T(8,128)(2,1)} %v_ref.1, f32[8,128]{1,0:T(8,128)} %g_ref.1, f32[8,128,128]{2,1,0:T(8,128)} %wq_hbm.1, f32[8,128,128]{2,1,0:T(8,128)} %wk_hbm.1, ...), custom_call_target="tpu_custom_call" | custom-call | tf_op jit(solution)/shard_map/distill/pallas_call | solution.py:575
  99.9 0.0 copy-start.1
  99.9 2.3 %slice_bitcast_fusion = (f32[8,128,128]{2,1,0:T(8,128)}, f32[8,128,128]{2,1,0:T(8,128)}) fusion(f32[2,8,128,128]{3,2,1,0:T(8,128)} %get-tuple-element.7), kind=kLoop, calls=%fused_computation | loop fusion | bytes 2097152 | tf_op jit(solution)/shard_map/squeeze | solution.py:626
  102.2 0.0 copy-done.1
  102.2 0.0 copy-start
  102.2 0.6 copy.14
  102.8 0.1 copy-done
  102.9 0.6 copy.15
Async XLA Ops:
  99.9 2.3 %copy-start.1 = (f32[8,13]{1,0:T(8,128)S(1)}, f32[8,13]{1,0:T(8,128)}, u32[]{:S(2)}) copy-start(f32[8,13]{1,0:T(8,128)} %get-tuple-element.18) | copy-start | bytes 1252
  102.2 0.7 copy-start

commit v2 on v1

--- a/solution.py
+++ b/solution.py
@@ -22,7 +22,7 @@
 WIDTH = 64 * HD
 SMALL = 24
 GATE_ROWS = 32
-VALUE_ROWS = 128 + GATE_ROWS
+KEY_ROWS = 128 + GATE_ROWS
 PIECE = 64 + 8
 HALF = HD // 2
 LOG2E = 1.4426950408889634
@@ -109,9 +109,9 @@
     tgt[h] += dg(jnp.concatenate([w0.astype(BF), w1.astype(BF)], axis=1), values, 1, 0)
 
 
-def level_weights(c, vals, lc, weights):
+def level_weights(c, keys_all, lc, weights):
     upper = (iota((TOK, TOK), 0) <= iota((TOK, TOK), 1)).astype(BF)
-    lc[...] = dg(vals[:, TOK:].reshape(SPANS * GATE_ROWS, TOK), upper, 1, 0)
+    lc[...] = dg(keys_all[:, TOK:].reshape(SPANS * GATE_ROWS, TOK), upper, 1, 0)
 
     def step(i, since):
         x = c - 1 - i
@@ -224,10 +224,10 @@
 
 def whole_kernel(
     q_hbm, k_ref, v_ref, g_ref, wq_hbm, wk_hbm, lw, gain,
-    out, levels, gains,
+    done,
     qs, wq, wk, keys_all, vals, score, peak, total, tgt, lc, weights, ls, qp, kp, ks, comb, mix, sd, raw, res, local,
-    dstate, dquery, dkey, grads, pair, part, box, done, sums_box, small_part, small_pair, small_sum,
-    load, own_send, relay_send, twin_send, recv, sums_send, sums_recv, pair_send, pair_recv,
+    dstate, dquery, dkey, grads, pair, part, box, sums_box, small_part, small_pair, small_sum,
+    load, own_send, across_send, relay_send, twin_send, recv, sums_send, sums_recv, pair_send, pair_recv,
     part_send, part_recv, done_send, done_recv, small_sem,
 ):
     c = lax.axis_index("seq")
@@ -257,17 +257,18 @@
     loads.append(pltpu.make_async_copy(wk_hbm, wk, load.at[9]))
     for copy in loads:
         copy.start()
-    keys_all[c] = k_ref[...]
-    vals[c, :TOK] = v_ref[...]
-    vals[c, TOK:] = gate_pieces(g_ref[...])
+    keys_all[c, :TOK] = k_ref[...]
+    keys_all[c, TOK:] = gate_pieces(g_ref[...])
+    vals[c] = v_ref[...]
 
     @pl.when(k == 0)
     def _():
-        keys_all[c + 1] = jnp.zeros((TOK, HD), BF)
-        vals[c + 1] = jnp.zeros((VALUE_ROWS, HD), BF)
+        keys_all[c + 1] = jnp.zeros((KEY_ROWS, HD), BF)
+        vals[c + 1] = jnp.zeros((TOK, HD), BF)
 
     for copy in loads:
         copy.wait()
+    student_inside(qs, k_ref[...], g_ref[...], wq, wk, lw, qp, kp, mix, sd)
     pl.semaphore_wait(barrier, 23)
 
     def block(phase, slot):
@@ -280,8 +281,8 @@
     def to_twin(phase, slot):
         return copy_of(phase, slot, twin_send.at[phase, slot], twin)
 
-    def to_across(phase):
-        return copy_of(phase, c, own_send.at[phase, 0], across)
+    def to_across(phase, zs):
+        return copy_of(phase, at(0, zs, k), across_send.at[phase, zs], across)
 
     def to_row(phase, d):
         return copy_of(phase, c, own_send.at[phase, d], at(y, (z + d) % 8, k))
@@ -297,11 +298,13 @@
             else:
                 copy.start()
 
+    row_first = (y == 0) & (k == 0)
+
     def own_moves(phase, wait=False):
-        act(y == 0, to_across(phase), wait)
+        act(y == 0, to_across(phase, z), wait)
         act(k == 0, to_twin(phase, c), wait)
         for d in far_first:
-            act(z + d < 8, to_row(phase, d), wait)
+            act((z + d < 8) | row_first, to_row(phase, d), wait)
 
     def arrived(phase, slot):
         to_twin(phase, slot).wait_recv()
@@ -312,7 +315,7 @@
             slot = at(0, z, k)
             arrived(phase, slot)
             for d in far_first:
-                relayed(phase, d).start()
+                act(k == 1, relayed(phase, d))
             to_twin(phase, slot).start()
 
     def chip_of(i):
@@ -322,11 +325,12 @@
     def forward(phase, i):
         zs = chip_of(i)
 
-        @pl.when(zs < z)
+        @pl.when((zs < z) | row_first)
         def _():
             slot = at(y, zs, k)
             arrived(phase, slot)
-            to_twin(phase, slot).start()
+            act(row_first, to_across(phase, zs))
+            act(zs < z, to_twin(phase, slot))
 
         @pl.when(second)
         def _():
@@ -349,16 +353,15 @@
         lax.fori_loop(0, 2, one, 0)
 
     own_moves(0)
-    own_moves(1)
-    student_inside(qs, k_ref[...], g_ref[...], wq, wk, lw, qp, kp, mix, sd)
-    relay(0)
-    relay(1)
 
     @pl.when(k == 1)
     def _():
         arrived(0, c - 1)
 
     scored(c, own_pair, True, qs, keys_all, peak, score)
+    relay(0)
+    own_moves(1)
+    relay(1)
 
     def key_step(i, carry):
         @pl.when(i < 8)
@@ -369,12 +372,6 @@
         return carry
 
     lax.fori_loop(1, 9, key_step, 0)
-
-    def value_forward(i, carry):
-        forward(1, i)
-        return carry
-
-    lax.fori_loop(1, 8, value_forward, 0)
     for h in range(HEADS):
         peak[rows(h)] = jnp.broadcast_to(
             jnp.max(peak[rows(h)], axis=1, keepdims=True), (TOK, TOK)
@@ -382,10 +379,14 @@
     total[...] = jnp.zeros_like(total)
     tgt[...] = jnp.zeros_like(tgt)
     ls[...] = jnp.zeros_like(ls)
+    level_weights(c, keys_all, lc, weights)
 
     @pl.when(k == 1)
     def _():
         arrived(1, c - 1)
+        keys = keys_all[c - 1, :TOK].astype(F32).T
+        for h in range(HEADS):
+            ls[0, h] = mm_right_exact(keys * weights[c - 1, h : h + 1], vals[c - 1], 1, 0)
 
     level = local_levels()
     for h in range(HEADS):
@@ -395,29 +396,7 @@
             mask = jnp.where(level == j, lw[h, j], mask)
         local[h] = mm_right_exact(sd[h] * mask, v_ref[...], 1, 0)
 
-    def all_here(i, carry):
-        zs = jnp.where(i == 0, z, chip_of(i))
-
-        @pl.when(zs < z)
-        def _():
-            arrived(1, at(y, zs, 1 - k))
-
-        @pl.when(second)
-        def _():
-            arrived(1, at(0, zs, 1 - k))
-
-        return carry
-
-    lax.fori_loop(0, 8, all_here, 0)
-    level_weights(c, vals, lc, weights)
-
-    @pl.when(k == 1)
-    def _():
-        keys = keys_all[c - 1].astype(F32).T
-        for h in range(HEADS):
-            ls[0, h] = mm_right_exact(keys * weights[c - 1, h : h + 1], vals[c - 1, :TOK], 1, 0)
-
-    def use_values(p, carry):
+    def use_values(p):
         values = pair_of(vals, p)
         keys = pair_of(keys_all, p).astype(F32).T
         weight = jnp.concatenate([weights[2 * p], weights[2 * p + 1]], axis=1)
@@ -427,9 +406,16 @@
         for h in range(HEADS):
             weighed(p, h, values, score, peak, total, tgt)
             ls[j, h] += mm_right_exact(keys * weight[h : h + 1], values, 1, 0)
+
+    def value_step(i, carry):
+        @pl.when(i < 8)
+        def _():
+            forward(1, i)
+
+        pairs(1, i - 1, use_values)
         return carry
 
-    lax.fori_loop(0, own_pair, use_values, 0)
+    lax.fori_loop(1, 9, value_step, 0)
     for h in range(HEADS):
         tgt[h] = tgt[h] / jnp.sum(total[rows(h)], axis=1, keepdims=True)
     entry = jnp.exp(column_cumulative(g_ref[...]))
@@ -520,30 +506,20 @@
                 sum_from(h, a).wait_recv()
                 sum_twin(k, h, a).start()
 
-    for a in range(2):
-        out[k, :, a * HALF : (a + 1) * HALF] = done[k, :, a, :HALF]
-    tile = jnp.concatenate(
-        [done[k, t, 0, HALF:] for t in range(2)] + [jnp.zeros((TOK - 16, TOK), F32)], axis=0
-    ).T
-    levels[...] = tile[:HEADS, :LEVELS]
-    gains[...] = done[k, 2, 0, HALF:]
     for h in range(8):
         for a in range(2):
             sum_twin(1 - k, h, a).wait_recv()
-    for a in range(2):
-        out[1 - k, :, a * HALF : (a + 1) * HALF] = done[1 - k, :, a, :HALF]
 
     for phase in range(2):
         own_moves(phase, True)
 
-        @pl.when(second)
-        def _(phase=phase):
-            for d in far_first:
-                relayed(phase, d).wait_send()
-            to_twin(phase, at(0, z, k)).wait_send()
+        for d in far_first:
+            act(second & (k == 1), relayed(phase, d), True)
+        act(second, to_twin(phase, at(0, z, k)), True)
 
         def sent(i, carry, phase=phase):
             zs = chip_of(i)
+            act(row_first, to_across(phase, zs), True)
             act(zs < z, to_twin(phase, at(y, zs, k)), True)
             act(second, to_twin(phase, at(0, zs, k)), True)
             return carry
@@ -559,6 +535,17 @@
             sum_twin(k, h, a).wait_send()
 
 
+def written_kernel(done, grad_query, grad_key, levels, gains):
+    for which, ref in enumerate((grad_query, grad_key)):
+        for a in range(2):
+            ref[:, a * HALF : (a + 1) * HALF] = done[which, :, a, :HALF]
+    tile = jnp.concatenate(
+        [done[0, t, 0, HALF:] for t in range(2)] + [jnp.zeros((TOK - 16, TOK), F32)], axis=0
+    ).T
+    levels[...] = tile[:HEADS, :LEVELS]
+    gains[...] = done[0, 2, 0, HALF:]
+
+
 VM = pl.BlockSpec(memory_space=pltpu.VMEM)
 SM = pl.BlockSpec(memory_space=pltpu.SMEM)
 ANY = pl.BlockSpec(memory_space=pl.ANY)
@@ -572,17 +559,17 @@
 def on_device(queries, key_vectors, value_vectors, log_gate, query_map, key_map, lw, norm_gain):
     matrix = pltpu.VMEM((HEADS, TOK, HD), F32)
     small = pltpu.VMEM((SMALL, TOK), F32)
-    out, levels, gains = pl.pallas_call(
+    done = pl.pallas_call(
         whole_kernel,
-        out_shape=(shaped((2, HEADS, HD, HD)), shaped((HEADS, LEVELS)), shaped((HEADS, HD))),
+        out_shape=shaped((2, HEADS, 2, PIECE, HD)),
         in_specs=[ANY, VM, VM, VM, ANY, ANY, SM, VM],
-        out_specs=(VM,) * 3,
+        out_specs=VM,
         scratch_shapes=[
             pltpu.VMEM((HEADS * TOK, HD), BF),
             matrix,
             matrix,
+            pltpu.VMEM((SPANS, KEY_ROWS, HD), BF),
             pltpu.VMEM((SPANS, TOK, HD), BF),
-            pltpu.VMEM((SPANS, VALUE_ROWS, HD), BF),
             pltpu.VMEM((SPANS // 2, HEADS * TOK, 2 * TOK), F32),
             pltpu.VMEM((HEADS * TOK, TOK), F32),
             pltpu.VMEM((HEADS * TOK, TOK), F32),
@@ -595,12 +582,12 @@
             matrix,
             pltpu.VMEM((HEADS, 2, PIECE, HD), F32),
             pltpu.VMEM((16, PIECE, HD), F32),
-            pltpu.VMEM((2, HEADS, 2, PIECE, HD), F32),
             pltpu.VMEM((HEADS, 8, TOK), F32),
             small,
             small,
             small,
             DMA((10,)),
+            DMA((2, 8)),
             DMA((2, 8)),
             DMA((2, 8)),
             DMA((2, SPANS)),
@@ -623,7 +610,19 @@
         queries, key_vectors, value_vectors, log_gate, query_map, key_map, lw,
         norm_gain.reshape(HEADS, HD),
     )
-    return out[0], out[1], levels, gains.reshape(-1)
+    grad_query, grad_key, levels, gains = pl.pallas_call(
+        written_kernel,
+        out_shape=(
+            shaped((HEADS, HD, HD)),
+            shaped((HEADS, HD, HD)),
+            shaped((HEADS, LEVELS)),
+            shaped((HEADS, HD)),
+        ),
+        in_specs=[VM],
+        out_specs=(VM,) * 4,
+        name="written",
+    )(done)
+    return grad_query, grad_key, levels, gains.reshape(-1)
 
 
 def solution(mesh):

time: 104 us -> 95.9 us (0.922)
  Pallas kernels: 99.3 us -> 95 us
  local copies, waits for them, and re-layouts: 3.55 us -> 0 us
    pallas_call x1 -> x2, Pallas kernels: 99.3 us -> 95 us  [the longest x1 92.8 us: on_device(): pl.pallas_call(whole_kernel, out_shape=shaped((2, HEADS, 2, PIECE, HD)),...]
    squeeze x1 -> x0, local copies, waits for them, and re-layouts: 2.27 us -> none  [on_device(): return (out[0], out[1], levels, gains.reshape(-1))]
    unnamed x6 -> x0, local copies, waits for them, and re-layouts: 1.28 us -> none
where the time goes in v2:
time: 95.9 us; the launch traced here: 95.7 us
  Pallas kernels  95 us (99%)
    pallas_call x1, Pallas kernels, on_device(): pl.pallas_call(whole_kernel, out_shape=shaped((2, HEADS, 2, PIECE, HD)),...  92.8 us
    pallas_call x1, Pallas kernels, on_device(): pl.pallas_call(written_kernel, out_shape=(shaped((HEADS, HD, HD)), shaped...  2.28 us

profile of v2, /device:TPU:1, one launch (start us, length us, event | category | flops | bytes accessed | tf_op | source)
XLA Modules:
  0.0 95.7 jit_solution(12341549064596767381)
XLA Ops:
  0.6 92.8 %distill.1.done = f32[2,8,2,72,128]{4,3,2,1,0:T(8,128)} custom-call(bf16[128,1024]{1,0:T(8,128)(2,1)} %q_hbm.1, bf16[128,128]{1,0:T(8,128)(2,1)} %k_ref.1, bf16[128,128]{1,0:T(8,128)(2,1)} %v_ref.1, f32[8,128]{1,0:T(8,128)} %g_ref.1, f32[8,128,128]{2,1,0:T(8,128)} %wq_hbm.1, f32[8,128,128]{2,1,0:T(8,128)} %wk_hbm.1, f32[8,13]{1,0:T(8,128)} %lw.1, ...), custom_call_target="tpu_custom_call" | custom-call | tf_op jit(solution)/shard_map/distill/pallas_call | solution.py:562
  93.4 2.3 %written.1 = (f32[8,128,128]{2,1,0:T(8,128)}, f32[8,128,128]{2,1,0:T(8,128)}, f32[8,13]{1,0:T(8,128)}, f32[8,128]{1,0:T(8,128)}) custom-call(f32[2,8,2,72,128]{4,3,2,1,0:T(8,128)} %distill.1.done), custom_call_target="tpu_custom_call" | custom-call | tf_op jit(solution)/shard_map/written/pallas_call | solution.py:613

commit v3 on v2

--- a/solution.py
+++ b/solution.py
@@ -23,8 +23,7 @@
 SMALL = 24
 GATE_ROWS = 32
 KEY_ROWS = 128 + GATE_ROWS
-PIECE = 64 + 8
-HALF = HD // 2
+PIECE = 128 + 8
 LOG2E = 1.4426950408889634
 SCALE = HD**-0.5 * LOG2E
 LIMIT = 58 << 20
@@ -226,26 +225,22 @@
     q_hbm, k_ref, v_ref, g_ref, wq_hbm, wk_hbm, lw, gain,
     done,
     qs, wq, wk, keys_all, vals, score, peak, total, tgt, lc, weights, ls, qp, kp, ks, comb, mix, sd, raw, res, local,
-    dstate, dquery, dkey, grads, pair, part, box, sums_box, small_part, small_pair, small_sum,
+    dstate, dquery, dkey, grads, pair, part, box, mine, far, sums_box, small_part, small_pair, small_sum,
     load, own_send, across_send, relay_send, twin_send, recv, sums_send, sums_recv, pair_send, pair_recv,
-    part_send, part_recv, done_send, done_recv, small_sem,
+    part_send, part_recv, done_send, done_recv, small_sem, swap_sem,
 ):
     c = lax.axis_index("seq")
     y, z, k = c // 16, c // 2 % 8, c % 2
     own_pair = c // 2
     second = y == 1
     twin, across = at(y, z, 1 - k), at(1 - y, z, k)
-    far_first = (4, 3, 5, 2, 6, 1, 7)
+    row_order = (1, 2, 3, 4, 5, 6, 7)
     me = lax.axis_index("head")
     head_peers = [(me + d) % HEADS for d in range(1, HEADS)]
 
     barrier = pltpu.get_barrier_semaphore()
-    for d in range(8):
-        for other in range(2):
-            if d or other:
-                target = at((y + other) % 2, (z + d) % 8, k)
-                pl.semaphore_signal(barrier, inc=1, device_id={"seq": target}, device_id_type=MESH)
-    pl.semaphore_signal(barrier, inc=1, device_id={"seq": twin}, device_id_type=MESH)
+    for target in [twin, across] + [at(y, (z + d) % 8, k) for d in range(1, 8)]:
+        pl.semaphore_signal(barrier, inc=1, device_id={"seq": target}, device_id_type=MESH)
     for peer in head_peers:
         pl.semaphore_signal(barrier, inc=1, device_id={"head": peer}, device_id_type=MESH)
 
@@ -269,7 +264,7 @@
     for copy in loads:
         copy.wait()
     student_inside(qs, k_ref[...], g_ref[...], wq, wk, lw, qp, kp, mix, sd)
-    pl.semaphore_wait(barrier, 23)
+    pl.semaphore_wait(barrier, 16)
 
     def block(phase, slot):
         return keys_all.at[slot] if phase == 0 else vals.at[slot]
@@ -303,7 +298,7 @@
     def own_moves(phase, wait=False):
         act(y == 0, to_across(phase, z), wait)
         act(k == 0, to_twin(phase, c), wait)
-        for d in far_first:
+        for d in row_order:
             act((z + d < 8) | row_first, to_row(phase, d), wait)
 
     def arrived(phase, slot):
@@ -314,7 +309,7 @@
         def _():
             slot = at(0, z, k)
             arrived(phase, slot)
-            for d in far_first:
+            for d in row_order:
                 act(k == 1, relayed(phase, d))
             to_twin(phase, slot).start()
 
@@ -427,6 +422,21 @@
     ]
     for copy in outgoing:
         copy.start()
+    for phase in range(2):
+        own_moves(phase, True)
+
+        for d in row_order:
+            act(second & (k == 1), relayed(phase, d), True)
+        act(second, to_twin(phase, at(0, z, k)), True)
+
+        def sent(i, carry, phase=phase):
+            zs = chip_of(i)
+            act(row_first, to_across(phase, zs), True)
+            act(zs < z, to_twin(phase, at(y, zs, k)), True)
+            act(second, to_twin(phase, at(0, zs, k)), True)
+            return carry
+
+        lax.fori_loop(1, 8, sent, 0)
     for d, peer in enumerate(head_peers):
         remote(
             "head", sums_box.at[peer], sums_box.at[peer], sums_send.at[d], sums_recv.at[peer], peer
@@ -440,7 +450,7 @@
 
     small_twin = remote("seq", small_part, small_pair, small_sem.at[0], small_sem.at[1], twin)
     small_twin.start()
-    order = [(z + d) % 8 for d in far_first + (0,)]
+    order = [(z + d) % 8 for d in range(1, 9)]
 
     def twin_part(h):
         return remote("seq", grads.at[1 - k, h], pair.at[h], pair_send.at[h], pair_recv.at[h], twin)
@@ -452,98 +462,74 @@
         twin_part(h).start()
     small_twin.wait_recv()
     small_sum[...] = small_part[...] + small_pair[...]
-    here = y * 8 + z
-
-    def piece_to(h, a):
-        return remote(
-            "seq", part.at[h, a], box.at[here], part_send.at[h, a], part_recv.at[here], at(a, h, k)
-        )
-
-    for h in order:
+
+    def piece_to(d, h):
+        return remote("seq", part.at[h], box.at[z], part_send.at[d], part_recv.at[z], at(y, h, k))
+
+    def piece_from(d, h):
+        return remote("seq", part.at[h], box.at[h], part_send.at[d], part_recv.at[h], at(y, h, k))
+
+    def own_piece(h):
+        tile = pl.multiple_of(h % 3 * 8, 8)
+        return jnp.concatenate([grads[k, h] + pair[h], small_sum[pl.ds(tile, 8)]], axis=0)
+
+    for d, h in enumerate(order):
         twin_part(h).wait_recv()
-        tile = h % 3
-        for a in range(2):
-            part[h, a, :HALF] = grads[k, h, a * HALF : (a + 1) * HALF] + pair[h, a * HALF : (a + 1) * HALF]
-            part[h, a, HALF:] = small_sum[pl.ds(pl.multiple_of(tile * 8, 8), 8)]
-            act((h != z) | (a != y), piece_to(h, a))
-    box[here] = part[z, y]
-    for h in order:
-        for a in range(2):
-            source = a * 8 + h
-
-            @pl.when((h != z) | (a != y))
-            def _(source=source, h=h, a=a):
-                remote(
-                    "seq", part.at[h, a], box.at[source], part_send.at[h, a], part_recv.at[source], at(a, h, k)
-                ).wait_recv()
-
-    whole = box[0]
-    for i in range(1, 16):
-        whole = whole + box[i]
-    done[k, z, y] = whole
-
-    def sum_to(h, a):
-        ref = done.at[k, z, y]
-        return remote("seq", ref, ref, done_send.at[0, h, a], done_recv.at[0, z, y], at(a, h, k))
-
-    def sum_from(h, a):
-        ref = done.at[k, h, a]
-        return remote("seq", ref, ref, done_send.at[0, h, a], done_recv.at[0, h, a], at(a, h, k))
-
-    def sum_twin(core, h, a):
-        ref = done.at[core, h, a]
-        return remote("seq", ref, ref, done_send.at[1, h, a], done_recv.at[1, h, a], twin)
-
-    for h in order:
-        for a in range(2):
-            act((h != z) | (a != y), sum_to(h, a))
-    sum_twin(k, z, y).start()
-    for h in [(z + d) % 8 for d in (0, 1, 7, 2, 6, 3, 5, 4)]:
-        for a in range(2):
-
-            @pl.when((h != z) | (a != y))
-            def _(h=h, a=a):
-                sum_from(h, a).wait_recv()
-                sum_twin(k, h, a).start()
-
-    for h in range(8):
-        for a in range(2):
-            sum_twin(1 - k, h, a).wait_recv()
-
-    for phase in range(2):
-        own_moves(phase, True)
-
-        for d in far_first:
-            act(second & (k == 1), relayed(phase, d), True)
-        act(second, to_twin(phase, at(0, z, k)), True)
-
-        def sent(i, carry, phase=phase):
-            zs = chip_of(i)
-            act(row_first, to_across(phase, zs), True)
-            act(zs < z, to_twin(phase, at(y, zs, k)), True)
-            act(second, to_twin(phase, at(0, zs, k)), True)
-            return carry
-
-        lax.fori_loop(1, 8, sent, 0)
-    for copy in outgoing + [small_twin]:
-        copy.wait_send()
+        if d < 7:
+            part[h] = own_piece(h)
+            piece_to(d, h).start()
+        else:
+            box[h] = own_piece(h)
     for h in order:
         twin_part(h).wait_send()
-        for a in range(2):
-            act((h != z) | (a != y), piece_to(h, a), True)
-            act((h != z) | (a != y), sum_to(h, a), True)
-            sum_twin(k, h, a).wait_send()
+    for d, h in enumerate(order[:7]):
+        piece_from(d, h).wait_recv()
+    whole = box[0]
+    for i in range(1, 8):
+        whole = whole + box[i]
+    mine[...] = whole
+    swap = remote("seq", mine, far, swap_sem.at[0], swap_sem.at[1], across)
+    swap.start()
+    for d, h in enumerate(order[:7]):
+        piece_to(d, h).wait_send()
+    swap.wait_recv()
+    done[k, z] = mine[...] + far[...]
+
+    def sum_to(d):
+        ref = done.at[k, z]
+        return remote("seq", ref, ref, done_send.at[0, d], done_recv.at[0, z], at(y, (z + d + 1) % 8, k))
+
+    def sum_from(d, h):
+        ref = done.at[k, h]
+        return remote("seq", ref, ref, done_send.at[0, d], done_recv.at[0, h], at(y, h, k))
+
+    def sum_twin(core, h):
+        ref = done.at[core, h]
+        return remote("seq", ref, ref, done_send.at[1, h], done_recv.at[1, h], twin)
+
+    for d in range(7):
+        sum_to(d).start()
+    sum_twin(k, z).start()
+    for d in (0, 6, 1, 5, 2, 4, 3):
+        sum_from(d, order[d]).wait_recv()
+        sum_twin(k, order[d]).start()
+    for h in range(8):
+        sum_twin(1 - k, h).wait_recv()
+    for copy in outgoing + [small_twin, swap, sum_twin(k, z)]:
+        copy.wait_send()
+    for d, h in enumerate(order[:7]):
+        sum_to(d).wait_send()
+        sum_twin(k, h).wait_send()
 
 
 def written_kernel(done, grad_query, grad_key, levels, gains):
-    for which, ref in enumerate((grad_query, grad_key)):
-        for a in range(2):
-            ref[:, a * HALF : (a + 1) * HALF] = done[which, :, a, :HALF]
+    grad_query[...] = done[0, :, :HD]
+    grad_key[...] = done[1, :, :HD]
     tile = jnp.concatenate(
-        [done[0, t, 0, HALF:] for t in range(2)] + [jnp.zeros((TOK - 16, TOK), F32)], axis=0
+        [done[0, t, HD:] for t in range(2)] + [jnp.zeros((TOK - 16, TOK), F32)], axis=0
     ).T
     levels[...] = tile[:HEADS, :LEVELS]
-    gains[...] = done[0, 2, 0, HALF:]
+    gains[...] = done[0, 2, HD:]
 
 
 VM = pl.BlockSpec(memory_space=pltpu.VMEM)
@@ -561,7 +547,7 @@
     small = pltpu.VMEM((SMALL, TOK), F32)
     done = pl.pallas_call(
         whole_kernel,
-        out_shape=shaped((2, HEADS, 2, PIECE, HD)),
+        out_shape=shaped((2, HEADS, PIECE, HD)),
         in_specs=[ANY, VM, VM, VM, ANY, ANY, SM, VM],
         out_specs=VM,
         scratch_shapes=[
@@ -580,8 +566,10 @@
             *[matrix] * 12,
             pltpu.VMEM((2, HEADS, HD, HD), F32),
             matrix,
-            pltpu.VMEM((HEADS, 2, PIECE, HD), F32),
-            pltpu.VMEM((16, PIECE, HD), F32),
+            pltpu.VMEM((HEADS, PIECE, HD), F32),
+            pltpu.VMEM((8, PIECE, HD), F32),
+            pltpu.VMEM((PIECE, HD), F32),
+            pltpu.VMEM((PIECE, HD), F32),
             pltpu.VMEM((HEADS, 8, TOK), F32),
             small,
             small,
@@ -596,10 +584,11 @@
             DMA((HEADS,)),
             DMA((8,)),
             DMA((8,)),
-            DMA((8, 2)),
-            DMA((16,)),
-            DMA((2, 8, 2)),
-            DMA((2, 8, 2)),
+            DMA((7,)),
+            DMA((8,)),
+            DMA((2, 8)),
+            DMA((2, 8)),
+            DMA((2,)),
             DMA((2,)),
         ],
         compiler_params=pltpu.CompilerParams(

time: 95.9 us -> 96.1 us (level)
  no operation moved by 1% of the time
where the time goes in v3:
time: 96.1 us; the launch traced here: 95.9 us
  Pallas kernels  95.3 us (99%)
    pallas_call x1, Pallas kernels, on_device(): pl.pallas_call(whole_kernel, out_shape=shaped((2, HEADS, PIECE, HD)), in_...  93 us
    pallas_call x1, Pallas kernels, on_device(): pl.pallas_call(written_kernel, out_shape=(shaped((HEADS, HD, HD)), shaped...  2.25 us

profile of v3, /device:TPU:1, one launch (start us, length us, event | category | flops | bytes accessed | tf_op | source)
XLA Modules:
  0.0 95.9 jit_solution(5899530880103723763)
XLA Ops:
  0.6 93.0 %distill.1.done = f32[2,8,136,128]{3,2,1,0:T(8,128)} custom-call(bf16[128,1024]{1,0:T(8,128)(2,1)} %q_hbm.1, bf16[128,128]{1,0:T(8,128)(2,1)} %k_ref.1, bf16[128,128]{1,0:T(8,128)(2,1)} %v_ref.1, f32[8,128]{1,0:T(8,128)} %g_ref.1, f32[8,128,128]{2,1,0:T(8,128)} %wq_hbm.1, f32[8,128,128]{2,1,0:T(8,128)} %wk_hbm.1, f32[8,13]{1,0:T(8,128)} %lw.1, f32[8,128]{1,0:T(8,128)} %bitcast.2), custom_call_target="tpu_custom_call" | custom-call | tf_op jit(solution)/shard_map/distill/pallas_call | solution.py:548
  93.7 2.3 %written.1 = (f32[8,128,128]{2,1,0:T(8,128)}, f32[8,128,128]{2,1,0:T(8,128)}, f32[8,13]{1,0:T(8,128)}, f32[8,128]{1,0:T(8,128)}) custom-call(f32[2,8,136,128]{3,2,1,0:T(8,128)} %distill.1.done), custom_call_target="tpu_custom_call" | custom-call | tf_op jit(solution)/shard_map/written/pallas_call | solution.py:602

commit v4 on v3

--- a/solution.py
+++ b/solution.py
@@ -227,7 +227,7 @@
     qs, wq, wk, keys_all, vals, score, peak, total, tgt, lc, weights, ls, qp, kp, ks, comb, mix, sd, raw, res, local,
     dstate, dquery, dkey, grads, pair, part, box, mine, far, sums_box, small_part, small_pair, small_sum,
     load, own_send, across_send, relay_send, twin_send, recv, sums_send, sums_recv, pair_send, pair_recv,
-    part_send, part_recv, done_send, done_recv, small_sem, swap_sem,
+    part_send, part_recv, done_send, done_recv, both_send, both_recv, small_sem, swap_send, swap_recv,
 ):
     c = lax.axis_index("seq")
     y, z, k = c // 16, c // 2 % 8, c % 2
@@ -450,7 +450,7 @@
 
     small_twin = remote("seq", small_part, small_pair, small_sem.at[0], small_sem.at[1], twin)
     small_twin.start()
-    order = [(z + d) % 8 for d in range(1, 9)]
+    order = [(z + d) % 8 for d in (4, 3, 5, 1, 7, 2, 6, 0)]
 
     def twin_part(h):
         return remote("seq", grads.at[1 - k, h], pair.at[h], pair_send.at[h], pair_recv.at[h], twin)
@@ -463,62 +463,115 @@
     small_twin.wait_recv()
     small_sum[...] = small_part[...] + small_pair[...]
 
-    def piece_to(d, h):
-        return remote("seq", part.at[h], box.at[z], part_send.at[d], part_recv.at[z], at(y, h, k))
-
-    def piece_from(d, h):
-        return remote("seq", part.at[h], box.at[h], part_send.at[d], part_recv.at[h], at(y, h, k))
-
-    def own_piece(h):
+    def lines(a):
+        return pl.ds(0, 64) if a == 0 else pl.ds(64, PIECE - 64)
+
+    def chip(d):
+        return (z + 8 + d) % 8
+
+    def piece(n, a):
+        lean = 1 - 2 * a
+        chunk, target = ((-4, -2), (-3, -1), (3, 1), (-1, -1), (1, 1), (-2, -2), (2, 2))[n]
+        return remote(
+            "seq", part.at[chip(lean * chunk), lines(a)], box.at[n, lines(a)], part_send.at[a, n],
+            part_recv.at[a, n], at(y, chip(lean * target), k),
+        )
+
+    def ready(h):
+        twin_part(h).wait_recv()
         tile = pl.multiple_of(h % 3 * 8, 8)
-        return jnp.concatenate([grads[k, h] + pair[h], small_sum[pl.ds(tile, 8)]], axis=0)
-
-    for d, h in enumerate(order):
-        twin_part(h).wait_recv()
-        if d < 7:
-            part[h] = own_piece(h)
-            piece_to(d, h).start()
-        else:
-            box[h] = own_piece(h)
+        part[h, :HD] = grads[k, h] + pair[h]
+        part[h, HD:] = small_sum[pl.ds(tile, 8)]
+
+    ready(order[0])
+    for a in range(2):
+        piece(0, a).start()
+    ready(order[1])
+    ready(order[2])
+    for a in range(2):
+        piece(1, a).start()
+        piece(2, a).start()
+    ready(order[3])
+    ready(order[4])
+    for a in range(2):
+        piece(3, a).start()
+        piece(4, a).start()
+    for h in order[5:]:
+        ready(h)
     for h in order:
         twin_part(h).wait_send()
-    for d, h in enumerate(order[:7]):
-        piece_from(d, h).wait_recv()
-    whole = box[0]
-    for i in range(1, 8):
-        whole = whole + box[i]
-    mine[...] = whole
-    swap = remote("seq", mine, far, swap_sem.at[0], swap_sem.at[1], across)
-    swap.start()
-    for d, h in enumerate(order[:7]):
-        piece_to(d, h).wait_send()
-    swap.wait_recv()
-    done[k, z] = mine[...] + far[...]
-
-    def sum_to(d):
-        ref = done.at[k, z]
-        return remote("seq", ref, ref, done_send.at[0, d], done_recv.at[0, z], at(y, (z + d + 1) % 8, k))
-
-    def sum_from(d, h):
-        ref = done.at[k, h]
-        return remote("seq", ref, ref, done_send.at[0, d], done_recv.at[0, h], at(y, h, k))
+    for a in range(2):
+        lean = 1 - 2 * a
+        piece(0, a).wait_recv()
+        piece(1, a).wait_recv()
+        part[chip(-2 * lean), lines(a)] += box[0, lines(a)] + box[1, lines(a)]
+        piece(5, a).start()
+        piece(2, a).wait_recv()
+        part[chip(2 * lean), lines(a)] += box[2, lines(a)]
+        piece(6, a).start()
+
+    def swap(a):
+        return remote(
+            "seq", mine.at[lines(a)], far.at[lines(a)], swap_send.at[a], swap_recv.at[a], across
+        )
+
+    for a in range(2):
+        whole = part[z, lines(a)]
+        for n in range(3, 7):
+            piece(n, a).wait_recv()
+            whole = whole + box[n, lines(a)]
+        mine[lines(a)] = whole
+        swap(a).start()
+    for a in range(2):
+        for n in range(7):
+            piece(n, a).wait_send()
+
+    def spread(n, a):
+        lean = 1 - 2 * a
+        source, target = ((0, 2), (0, -2), (0, 1), (0, -1), (-2, 1), (-2, 2), (2, -1))[n]
+        h = chip(lean * source)
+        ref = done.at[k, h, lines(a)]
+        return remote(
+            "seq", ref, ref, done_send.at[a, n], done_recv.at[h, a], at(y, chip(lean * target), k)
+        )
+
+    def came(d, a):
+        h = chip(d)
+        ref = done.at[k, h, lines(a)]
+        return remote("seq", ref, ref, done_send.at[a, 0], done_recv.at[h, a], twin)
 
     def sum_twin(core, h):
         ref = done.at[core, h]
-        return remote("seq", ref, ref, done_send.at[1, h], done_recv.at[1, h], twin)
-
-    for d in range(7):
-        sum_to(d).start()
+        return remote("seq", ref, ref, both_send.at[h], both_recv.at[h], twin)
+
+    for a in range(2):
+        swap(a).wait_recv()
+        done[k, z, lines(a)] = mine[lines(a)] + far[lines(a)]
+        for n in range(4):
+            spread(n, a).start()
     sum_twin(k, z).start()
-    for d in (0, 6, 1, 5, 2, 4, 3):
-        sum_from(d, order[d]).wait_recv()
-        sum_twin(k, order[d]).start()
+    for a in range(2):
+        lean = 1 - 2 * a
+        came(-2 * lean, a).wait_recv()
+        spread(4, a).start()
+        spread(5, a).start()
+        came(2 * lean, a).wait_recv()
+        spread(6, a).start()
+    for d in (2, -2):
+        sum_twin(k, chip(d)).start()
+    for d in (1, -1, 3, -3, 4):
+        for a in range(2):
+            came(d, a).wait_recv()
+        sum_twin(k, chip(d)).start()
+    for copy in outgoing + [small_twin]:
+        copy.wait_send()
+    for a in range(2):
+        swap(a).wait_send()
+        for n in range(7):
+            spread(n, a).wait_send()
     for h in range(8):
         sum_twin(1 - k, h).wait_recv()
-    for copy in outgoing + [small_twin, swap, sum_twin(k, z)]:
-        copy.wait_send()
-    for d, h in enumerate(order[:7]):
-        sum_to(d).wait_send()
+    for h in order:
         sum_twin(k, h).wait_send()
 
 
@@ -567,7 +620,7 @@
             pltpu.VMEM((2, HEADS, HD, HD), F32),
             matrix,
             pltpu.VMEM((HEADS, PIECE, HD), F32),
-            pltpu.VMEM((8, PIECE, HD), F32),
+            pltpu.VMEM((7, PIECE, HD), F32),
             pltpu.VMEM((PIECE, HD), F32),
             pltpu.VMEM((PIECE, HD), F32),
             pltpu.VMEM((HEADS, 8, TOK), F32),
@@ -584,10 +637,13 @@
             DMA((HEADS,)),
             DMA((8,)),
             DMA((8,)),
-            DMA((7,)),
+            DMA((2, 7)),
+            DMA((2, 7)),
+            DMA((2, 7)),
+            DMA((8, 2)),
             DMA((8,)),
-            DMA((2, 8)),
-            DMA((2, 8)),
+            DMA((8,)),
+            DMA((2,)),
             DMA((2,)),
             DMA((2,)),
         ],

time: 96.1 us -> 89.6 us (0.932)
  Pallas kernels: 95.3 us -> 88.7 us
    pallas_call x1, Pallas kernels: 93 us -> 86.5 us  [on_device(): pl.pallas_call(whole_kernel, out_shape=shaped((2, HEADS, PIECE, HD)), in_...]
where the time goes in v4:
time: 89.6 us; the launch traced here: 89.4 us
  Pallas kernels  88.7 us (99%)
    pallas_call x1, Pallas kernels, on_device(): pl.pallas_call(whole_kernel, out_shape=shaped((2, HEADS, PIECE, HD)), in_...  86.5 us
    pallas_call x1, Pallas kernels, on_device(): pl.pallas_call(written_kernel, out_shape=(shaped((HEADS, HD, HD)), shaped...  2.25 us

profile of v4, /device:TPU:1, one launch (start us, length us, event | category | flops | bytes accessed | tf_op | source)
XLA Modules:
  0.0 89.4 jit_solution(13799153161437359695)
XLA Ops:
  0.6 86.5 %distill.1.done = f32[2,8,136,128]{3,2,1,0:T(8,128)} custom-call(bf16[128,1024]{1,0:T(8,128)(2,1)} %q_hbm.1, bf16[128,128]{1,0:T(8,128)(2,1)} %k_ref.1, bf16[128,128]{1,0:T(8,128)(2,1)} %v_ref.1, f32[8,128]{1,0:T(8,128)} %g_ref.1, f32[8,128,128]{2,1,0:T(8,128)} %wq_hbm.1, f32[8,128,128]{2,1,0:T(8,128)} %wk_hbm.1, f32[8,13]{1,0:T(8,128)} %lw.1, f32[8,128]{1,0:T(8,128)} %bitcast.2), custom_call_target="tpu_custom_call" | custom-call | tf_op jit(solution)/shard_map/distill/pallas_call | solution.py:601
  87.1 2.3 %written.1 = (f32[8,128,128]{2,1,0:T(8,128)}, f32[8,128,128]{2,1,0:T(8,128)}, f32[8,13]{1,0:T(8,128)}, f32[8,128]{1,0:T(8,128)}) custom-call(f32[2,8,136,128]{3,2,1,0:T(8,128)} %distill.1.done), custom_call_target="tpu_custom_call" | custom-call | tf_op jit(solution)/shard_map/written/pallas_call | solution.py:658

commit v5 on v4

--- a/solution.py
+++ b/solution.py
@@ -224,9 +224,9 @@
 def whole_kernel(
     q_hbm, k_ref, v_ref, g_ref, wq_hbm, wk_hbm, lw, gain,
     done,
-    qs, wq, wk, keys_all, vals, score, peak, total, tgt, lc, weights, ls, qp, kp, ks, comb, mix, sd, raw, res, local,
+    qs, wq, wk, keys_all, vals, scores, peak, total, tgt, lc, weights, ls, qp, kp, ks, comb, mix, sd, raw, res, local,
     dstate, dquery, dkey, grads, pair, part, box, mine, far, sums_box, small_part, small_pair, small_sum,
-    load, own_send, across_send, relay_send, twin_send, recv, sums_send, sums_recv, pair_send, pair_recv,
+    load, own_send, across_send, relay_send, onward_send, twin_send, recv, sums_send, sums_recv, pair_send, pair_recv,
     part_send, part_recv, done_send, done_recv, both_send, both_recv, small_sem, swap_send, swap_recv,
 ):
     c = lax.axis_index("seq")
@@ -234,12 +234,11 @@
     own_pair = c // 2
     second = y == 1
     twin, across = at(y, z, 1 - k), at(1 - y, z, k)
-    row_order = (1, 2, 3, 4, 5, 6, 7)
     me = lax.axis_index("head")
     head_peers = [(me + d) % HEADS for d in range(1, HEADS)]
 
     barrier = pltpu.get_barrier_semaphore()
-    for target in [twin, across] + [at(y, (z + d) % 8, k) for d in range(1, 8)]:
+    for target in [twin, across] + [at(y, (z + d) % 8, k) for d in (1, 2, 6, 7)]:
         pl.semaphore_signal(barrier, inc=1, device_id={"seq": target}, device_id_type=MESH)
     for peer in head_peers:
         pl.semaphore_signal(barrier, inc=1, device_id={"head": peer}, device_id_type=MESH)
@@ -264,7 +263,7 @@
     for copy in loads:
         copy.wait()
     student_inside(qs, k_ref[...], g_ref[...], wq, wk, lw, qp, kp, mix, sd)
-    pl.semaphore_wait(barrier, 16)
+    pl.semaphore_wait(barrier, 13)
 
     def block(phase, slot):
         return keys_all.at[slot] if phase == 0 else vals.at[slot]
@@ -279,11 +278,25 @@
     def to_across(phase, zs):
         return copy_of(phase, at(0, zs, k), across_send.at[phase, zs], across)
 
-    def to_row(phase, d):
-        return copy_of(phase, c, own_send.at[phase, d], at(y, (z + d) % 8, k))
-
-    def relayed(phase, d):
-        return copy_of(phase, at(0, z, k), relay_send.at[phase, d], at(y, (z + d) % 8, k))
+    lean_core = 1 - 2 * k
+    direct = (2, -2, 1, -1)
+
+    def chip_at(o):
+        return (z + 8 + lean_core * o) % 8
+
+    def source_at(o):
+        return (z + 8 - lean_core * o) % 8
+
+    def need(zs, o):
+        return (zs + 8 + lean_core * o) % 8 > zs
+
+    def wanted(zs, o):
+        if o == 2:
+            return need(zs, 2) | need(zs, 3) | need(zs, 4)
+        return need(zs, -2) | need(zs, -3) if o == -2 else need(zs, o)
+
+    def to_row(phase, slot, sem, o):
+        return copy_of(phase, slot, sem, at(y, chip_at(o), k))
 
     def act(when, copy, wait=False):
         @pl.when(when)
@@ -298,40 +311,54 @@
     def own_moves(phase, wait=False):
         act(y == 0, to_across(phase, z), wait)
         act(k == 0, to_twin(phase, c), wait)
-        for d in row_order:
-            act((z + d < 8) | row_first, to_row(phase, d), wait)
+        for n, o in enumerate(direct):
+            act(row_first | wanted(z, o), to_row(phase, c, own_send.at[phase, n], o), wait)
 
     def arrived(phase, slot):
         to_twin(phase, slot).wait_recv()
 
-    def relay(phase):
+    def relay(phase, wait=False):
         @pl.when(second)
         def _():
             slot = at(0, z, k)
-            arrived(phase, slot)
-            for d in row_order:
-                act(k == 1, relayed(phase, d))
-            to_twin(phase, slot).start()
+            if not wait:
+                arrived(phase, slot)
+            for n, o in enumerate(direct):
+                act(k == 1, to_row(phase, slot, relay_send.at[phase, n], o), wait)
+            act(second, to_twin(phase, slot), wait)
 
     def chip_of(i):
-        d = jnp.where(i % 2 == 1, (i + 1) // 2, 8 - i // 2)
-        return (z + 8 - d) % 8
-
-    def forward(phase, i):
-        zs = chip_of(i)
-
-        @pl.when((zs < z) | row_first)
+        far = jnp.where(i == 5, 3, jnp.where(i == 6, -3, 4))
+        near = jnp.where(i == 1, 2, jnp.where(i == 2, -2, jnp.where(i == 3, 1, -1)))
+        return source_at(jnp.where(i < 5, near, far))
+
+    def onward(o):
+        return ((0, 1), (1, 2)) if o == 2 else ((2, -1),) if o == -2 else ()
+
+    def forward_own(phase, zs, o=0, wait=False):
+        @pl.when(row_first | (wanted(zs, o) if o else zs < z))
         def _():
             slot = at(y, zs, k)
-            arrived(phase, slot)
-            act(row_first, to_across(phase, zs))
-            act(zs < z, to_twin(phase, slot))
-
+            if not wait:
+                arrived(phase, slot)
+            for n, step in onward(o):
+                act(
+                    row_first | need(zs, o + step),
+                    to_row(phase, slot, onward_send.at[phase, 0, n], step),
+                    wait,
+                )
+            act(row_first, to_across(phase, zs), wait)
+            act(zs < z, to_twin(phase, slot), wait)
+
+    def forward_other(phase, zs, o=0, wait=False):
         @pl.when(second)
         def _():
             slot = at(0, zs, k)
-            arrived(phase, slot)
-            to_twin(phase, slot).start()
+            if not wait:
+                arrived(phase, slot)
+            for n, step in onward(o):
+                act(k == 1, to_row(phase, slot, onward_send.at[phase, 1, n], step), wait)
+            act(second, to_twin(phase, slot), wait)
 
     def pairs(phase, i, use):
         zs = jnp.where(i == 0, z, chip_of(i))
@@ -353,20 +380,41 @@
     def _():
         arrived(0, c - 1)
 
-    scored(c, own_pair, True, qs, keys_all, peak, score)
+    scored(c, own_pair, True, qs, keys_all, peak, scores)
     relay(0)
     own_moves(1)
     relay(1)
 
+    def score(p):
+        scored(c, p, False, qs, keys_all, peak, scores)
+
+    for o in (2, -2):
+        forward_own(0, source_at(o), o)
+    pairs(0, 0, score)
+    for o in (2, -2):
+        forward_other(0, source_at(o), o)
+
     def key_step(i, carry):
         @pl.when(i < 8)
         def _():
-            forward(0, i)
-
-        pairs(0, i - 1, lambda p: scored(c, p, False, qs, keys_all, peak, score))
+            forward_own(0, chip_of(i))
+            forward_other(0, chip_of(i))
+
+        pairs(0, i - 2, score)
+
+        @pl.when(i == 5)
+        def _():
+            for o in (2, -2):
+                forward_own(1, source_at(o), o)
+
+        @pl.when(i == 7)
+        def _():
+            for o in (2, -2):
+                forward_other(1, source_at(o), o)
+
         return carry
 
-    lax.fori_loop(1, 9, key_step, 0)
+    lax.fori_loop(3, 10, key_step, 0)
     for h in range(HEADS):
         peak[rows(h)] = jnp.broadcast_to(
             jnp.max(peak[rows(h)], axis=1, keepdims=True), (TOK, TOK)
@@ -385,7 +433,7 @@
 
     level = local_levels()
     for h in range(HEADS):
-        weighed(own_pair, h, pair_of(vals, own_pair), score, peak, total, tgt)
+        weighed(own_pair, h, pair_of(vals, own_pair), scores, peak, total, tgt)
         mask = jnp.full((TOK, TOK), lw[h, 0], F32)
         for j in range(1, LOW + 1):
             mask = jnp.where(level == j, lw[h, j], mask)
@@ -399,18 +447,21 @@
         for b in range(4):
             j = j + (own_pair // (1 << b) != p // (1 << b)).astype(jnp.int32)
         for h in range(HEADS):
-            weighed(p, h, values, score, peak, total, tgt)
+            weighed(p, h, values, scores, peak, total, tgt)
             ls[j, h] += mm_right_exact(keys * weight[h : h + 1], values, 1, 0)
+
+    pairs(1, 0, use_values)
 
     def value_step(i, carry):
         @pl.when(i < 8)
         def _():
-            forward(1, i)
-
-        pairs(1, i - 1, use_values)
+            forward_own(1, chip_of(i))
+            forward_other(1, chip_of(i))
+
+        pairs(1, i - 2, use_values)
         return carry
 
-    lax.fori_loop(1, 9, value_step, 0)
+    lax.fori_loop(3, 10, value_step, 0)
     for h in range(HEADS):
         tgt[h] = tgt[h] / jnp.sum(total[rows(h)], axis=1, keepdims=True)
     entry = jnp.exp(column_cumulative(g_ref[...]))
@@ -425,18 +476,17 @@
     for phase in range(2):
         own_moves(phase, True)
 
-        for d in row_order:
-            act(second & (k == 1), relayed(phase, d), True)
-        act(second, to_twin(phase, at(0, z, k)), True)
+        relay(phase, True)
+        for o in direct[:2]:
+            forward_own(phase, source_at(o), o, True)
+            forward_other(phase, source_at(o), o, True)
 
         def sent(i, carry, phase=phase):
-            zs = chip_of(i)
-            act(row_first, to_across(phase, zs), True)
-            act(zs < z, to_twin(phase, at(y, zs, k)), True)
-            act(second, to_twin(phase, at(0, zs, k)), True)
+            forward_own(phase, chip_of(i), 0, True)
+            forward_other(phase, chip_of(i), 0, True)
             return carry
 
-        lax.fori_loop(1, 8, sent, 0)
+        lax.fori_loop(3, 8, sent, 0)
     for d, peer in enumerate(head_peers):
         remote(
             "head", sums_box.at[peer], sums_box.at[peer], sums_send.at[d], sums_recv.at[peer], peer
@@ -628,9 +678,10 @@
             small,
             small,
             DMA((10,)),
+            DMA((2, 4)),
             DMA((2, 8)),
-            DMA((2, 8)),
-            DMA((2, 8)),
+            DMA((2, 4)),
+            DMA((2, 2, 3)),
             DMA((2, SPANS)),
             DMA((2, SPANS)),
             DMA((7,)),

time: 89.6 us -> 80.9 us (0.903)
  Pallas kernels: 88.7 us -> 80 us
    pallas_call x1, Pallas kernels: 86.5 us -> 77.8 us  [on_device(): pl.pallas_call(whole_kernel, out_shape=shaped((2, HEADS, PIECE, HD)), in_...]
where the time goes in v5:
time: 80.9 us; the launch traced here: 80.7 us
  Pallas kernels  80 us (99%)
    pallas_call x1, Pallas kernels, on_device(): pl.pallas_call(whole_kernel, out_shape=shaped((2, HEADS, PIECE, HD)), in_...  77.8 us
    pallas_call x1, Pallas kernels, on_device(): pl.pallas_call(written_kernel, out_shape=(shaped((HEADS, HD, HD)), shaped...  2.25 us

profile of v5, /device:TPU:1, one launch (start us, length us, event | category | flops | bytes accessed | tf_op | source)
XLA Modules:
  0.0 80.7 jit_solution(13462608950240336450)
XLA Ops:
  0.6 77.8 %distill.1.done = f32[2,8,136,128]{3,2,1,0:T(8,128)} custom-call(bf16[128,1024]{1,0:T(8,128)(2,1)} %q_hbm.1, bf16[128,128]{1,0:T(8,128)(2,1)} %k_ref.1, bf16[128,128]{1,0:T(8,128)(2,1)} %v_ref.1, f32[8,128]{1,0:T(8,128)} %g_ref.1, f32[8,128,128]{2,1,0:T(8,128)} %wq_hbm.1, f32[8,128,128]{2,1,0:T(8,128)} %wk_hbm.1, f32[8,13]{1,0:T(8,128)} %lw.1, f32[8,128]{1,0:T(8,128)} %bitcast.2), custom_call_target="tpu_custom_call" | custom-call | tf_op jit(solution)/shard_map/distill/pallas_call | solution.py:651
  78.4 2.3 %written.1 = (f32[8,128,128]{2,1,0:T(8,128)}, f32[8,128,128]{2,1,0:T(8,128)}, f32[8,13]{1,0:T(8,128)}, f32[8,128]{1,0:T(8,128)}) custom-call(f32[2,8,136,128]{3,2,1,0:T(8,128)} %distill.1.done), custom_call_target="tpu_custom_call" | custom-call | tf_op jit(solution)/shard_map/written/pallas_call | solution.py:709

commit v6 on v5

--- a/solution.py
+++ b/solution.py
@@ -109,18 +109,18 @@
 
 
 def level_weights(c, keys_all, lc, weights):
-    upper = (iota((TOK, TOK), 0) <= iota((TOK, TOK), 1)).astype(BF)
-    lc[...] = dg(keys_all[:, TOK:].reshape(SPANS * GATE_ROWS, TOK), upper, 1, 0)
+    later = (iota((TOK, TOK), 0) > iota((TOK, TOK), 1)).astype(BF)
+    both = jnp.concatenate([later, jnp.ones((TOK, TOK), BF)], axis=1)
+    lc[...] = dg(keys_all[:, TOK:].reshape(SPANS * GATE_ROWS, TOK), both, 1, 0)
 
     def step(i, since):
         x = c - 1 - i
         three = lc[pl.ds(pl.multiple_of(x * GATE_ROWS, GATE_ROWS), 3 * HEADS)]
         own = three[:HEADS] + three[HEADS : 2 * HEADS] + three[2 * HEADS :]
-        since = since + own[:, TOK - 1 :]
-        weights[x] = jnp.exp(since - own)
-        return since
-
-    lax.fori_loop(0, c, step, jnp.zeros((HEADS, 1), F32))
+        weights[x] = jnp.exp(since + own[:, :TOK])
+        return since + own[:, TOK:]
+
+    lax.fori_loop(0, c, step, jnp.zeros((HEADS, TOK), F32))
 
 
 def gate_pieces(gate):
@@ -130,7 +130,7 @@
     return jnp.concatenate([high, middle, low, jnp.zeros_like(gate)], axis=0).astype(BF)
 
 
-def student_inside(qs, key, gate, wq, wk, lw, qp, kp, mix, sd):
+def student_inside(qs, key, value, gate, wq, wk, lw, qp, kp, mix, sd, local):
     upper = (iota((TOK, TOK), 0) <= iota((TOK, TOK), 1)).astype(F32)
     row_cum = dg(gate, upper, 1, 0, HIGHEST)
     col_cum = column_cumulative(gate)
@@ -148,6 +148,7 @@
             mask = jnp.where(level == j, lw[h, j], mask)
         sd[h] = mm(qp[h], kp[h], 1, 1) * decay
         mix[h] = decay * mask
+        local[h] = mm_right_exact(sd[h] * mask, value, 1, 0)
 
 
 def student_whole(entry, wk, lw, gain, ls, tgt, qp, ks, comb, raw, local):
@@ -262,7 +263,9 @@
 
     for copy in loads:
         copy.wait()
-    student_inside(qs, k_ref[...], g_ref[...], wq, wk, lw, qp, kp, mix, sd)
+    student_inside(
+        qs, k_ref[...], v_ref[...], g_ref[...], wq, wk, lw, qp, kp, mix, sd, local
+    )
     pl.semaphore_wait(barrier, 13)
 
     def block(phase, slot):
@@ -431,13 +434,8 @@
         for h in range(HEADS):
             ls[0, h] = mm_right_exact(keys * weights[c - 1, h : h + 1], vals[c - 1], 1, 0)
 
-    level = local_levels()
     for h in range(HEADS):
         weighed(own_pair, h, pair_of(vals, own_pair), scores, peak, total, tgt)
-        mask = jnp.full((TOK, TOK), lw[h, 0], F32)
-        for j in range(1, LOW + 1):
-            mask = jnp.where(level == j, lw[h, j], mask)
-        local[h] = mm_right_exact(sd[h] * mask, v_ref[...], 1, 0)
 
     def use_values(p):
         values = pair_of(vals, p)
@@ -505,11 +503,19 @@
     def twin_part(h):
         return remote("seq", grads.at[1 - k, h], pair.at[h], pair_send.at[h], pair_recv.at[h], twin)
 
-    for h in order:
+    def product(h):
         q_rows = qs[pl.ds(pl.multiple_of(h * TOK, TOK), TOK)]
         grads[0, h] = mm_left_exact(q_rows, dquery[h], 0, 0)
         grads[1, h] = mm(comb[h], dstate[h], 1, 1) + mm_left_exact(k_ref[...], dkey[h], 0, 0)
-        twin_part(h).start()
+
+    def products(heads):
+        for h in heads:
+            product(h)
+        for h in heads:
+            twin_part(h).start()
+
+    products(order[:3])
+    products(order[3:6])
     small_twin.wait_recv()
     small_sum[...] = small_part[...] + small_pair[...]
 
@@ -541,6 +547,7 @@
     for a in range(2):
         piece(1, a).start()
         piece(2, a).start()
+    products(order[6:])
     ready(order[3])
     ready(order[4])
     for a in range(2):
@@ -625,14 +632,20 @@
         sum_twin(k, h).wait_send()
 
 
-def written_kernel(done, grad_query, grad_key, levels, gains):
-    grad_query[...] = done[0, :, :HD]
-    grad_key[...] = done[1, :, :HD]
-    tile = jnp.concatenate(
-        [done[0, t, HD:] for t in range(2)] + [jnp.zeros((TOK - 16, TOK), F32)], axis=0
-    ).T
+def written_kernel(done, grad_query, grad_key, levels, gains, small, sems):
+    copies = [
+        pltpu.make_async_copy(done.at[0, :3, HD:], small, sems.at[0]),
+        pltpu.make_async_copy(done.at[0, :, :HD], grad_query, sems.at[1]),
+        pltpu.make_async_copy(done.at[1, :, :HD], grad_key, sems.at[2]),
+    ]
+    for copy in copies:
+        copy.start()
+    copies[0].wait()
+    tile = jnp.concatenate([small[0], small[1], jnp.zeros((TOK - 16, TOK), F32)], axis=0).T
     levels[...] = tile[:HEADS, :LEVELS]
-    gains[...] = done[0, 2, HD:]
+    gains[...] = small[2]
+    for copy in copies[1:]:
+        copy.wait()
 
 
 VM = pl.BlockSpec(memory_space=pltpu.VMEM)
@@ -663,7 +676,7 @@
             pltpu.VMEM((HEADS * TOK, TOK), F32),
             pltpu.VMEM((HEADS * TOK, TOK), F32),
             matrix,
-            pltpu.VMEM((SPANS * GATE_ROWS, TOK), F32),
+            pltpu.VMEM((SPANS * GATE_ROWS, 2 * TOK), F32),
             pltpu.VMEM((SPANS, HEADS, TOK), F32),
             pltpu.VMEM((CROSS, HEADS, HD, HD), F32),
             *[matrix] * 12,
@@ -714,8 +727,9 @@
             shaped((HEADS, LEVELS)),
             shaped((HEADS, HD)),
         ),
-        in_specs=[VM],
-        out_specs=(VM,) * 4,
+        in_specs=[ANY],
+        out_specs=(ANY, ANY, VM, VM),
+        scratch_shapes=[pltpu.VMEM((3, 8, TOK), F32), DMA((3,))],
         name="written",
     )(done)
     return grad_query, grad_key, levels, gains.reshape(-1)

time: 80.9 us -> 110 us (1.36)
  Pallas kernels: 80 us -> 109 us
    pallas_call x1, Pallas kernels: 2.25 us -> 33.5 us  [on_device(): pl.pallas_call(written_kernel, out_shape=(shaped((HEADS, HD, HD)), shaped...]
    pallas_call x1, Pallas kernels: 77.8 us -> 75.9 us  [on_device(): pl.pallas_call(whole_kernel, out_shape=shaped((2, HEADS, PIECE, HD)), in_...]
where the time goes in v6:
time: 110 us
  Pallas kernels  109 us (99%)
    pallas_call x1, Pallas kernels, on_device(): pl.pallas_call(whole_kernel, out_shape=shaped((2, HEADS, PIECE, HD)), in_...  75.9 us
    pallas_call x1, Pallas kernels, on_device(): pl.pallas_call(written_kernel, out_shape=(shaped((HEADS, HD, HD)), shaped...  33.5 us

profile of v6, /device:TPU:1, one launch (start us, length us, event | category | flops | bytes accessed | tf_op | source)
XLA Modules:
  0.0 110.1 jit_solution(14035060730409031815)
XLA Ops:
  0.6 75.9 %distill.1.done = f32[2,8,136,128]{3,2,1,0:T(8,128)} custom-call(bf16[128,1024]{1,0:T(8,128)(2,1)} %q_hbm.1, bf16[128,128]{1,0:T(8,128)(2,1)} %k_ref.1, bf16[128,128]{1,0:T(8,128)(2,1)} %v_ref.1, f32[8,128]{1,0:T(8,128)} %g_ref.1, f32[8,128,128]{2,1,0:T(8,128)} %wq_hbm.1, f32[8,128,128]{2,1,0:T(8,128)} %wk_hbm.1, f32[8,13]{1,0:T(8,128)} %lw.1, f32[8,128]{1,0:T(8,128)} %bitcast.2), custom_call_target="tpu_custom_call" | custom-call | tf_op jit(solution)/shard_map/distill/pallas_call | solution.py:664
  76.6 33.5 %written.1 = (f32[8,128,128]{2,1,0:T(8,128)}, f32[8,128,128]{2,1,0:T(8,128)}, f32[8,13]{1,0:T(8,128)}, f32[8,128]{1,0:T(8,128)}) custom-call(f32[2,8,136,128]{3,2,1,0:T(8,128)} %distill.1.done), custom_call_target="tpu_custom_call" | custom-call | tf_op jit(solution)/shard_map/written/pallas_call | solution.py:722

commit v7 on v6

--- a/solution.py
+++ b/solution.py
@@ -223,9 +223,9 @@
 
 
 def whole_kernel(
-    q_hbm, k_ref, v_ref, g_ref, wq_hbm, wk_hbm, lw, gain,
+    q_hbm, k_hbm, v_hbm, g_hbm, wq_hbm, wk_hbm, lw, gain_hbm,
     done,
-    qs, wq, wk, keys_all, vals, scores, peak, total, tgt, lc, weights, ls, qp, kp, ks, comb, mix, sd, raw, res, local,
+    k_ref, v_ref, g_ref, gain, qs, wq, wk, keys_all, vals, scores, peak, total, tgt, lc, weights, ls, qp, kp, ks, comb, mix, sd, raw, res, local,
     dstate, dquery, dkey, grads, pair, part, box, mine, far, sums_box, small_part, small_pair, small_sum,
     load, own_send, across_send, relay_send, onward_send, twin_send, recv, sums_send, sums_recv, pair_send, pair_recv,
     part_send, part_recv, done_send, done_recv, both_send, both_recv, small_sem, swap_send, swap_recv,
@@ -250,8 +250,12 @@
     ]
     loads.append(pltpu.make_async_copy(wq_hbm, wq, load.at[8]))
     loads.append(pltpu.make_async_copy(wk_hbm, wk, load.at[9]))
-    for copy in loads:
+    own = ((k_hbm, k_ref), (v_hbm, v_ref), (g_hbm, g_ref), (gain_hbm, gain))
+    first_loads = [pltpu.make_async_copy(a, b, load.at[10 + n]) for n, (a, b) in enumerate(own)]
+    for copy in first_loads + loads:
         copy.start()
+    for copy in first_loads:
+        copy.wait()
     keys_all[c, :TOK] = k_ref[...]
     keys_all[c, TOK:] = gate_pieces(g_ref[...])
     vals[c] = v_ref[...]
@@ -632,20 +636,14 @@
         sum_twin(k, h).wait_send()
 
 
-def written_kernel(done, grad_query, grad_key, levels, gains, small, sems):
-    copies = [
-        pltpu.make_async_copy(done.at[0, :3, HD:], small, sems.at[0]),
-        pltpu.make_async_copy(done.at[0, :, :HD], grad_query, sems.at[1]),
-        pltpu.make_async_copy(done.at[1, :, :HD], grad_key, sems.at[2]),
-    ]
-    for copy in copies:
-        copy.start()
-    copies[0].wait()
-    tile = jnp.concatenate([small[0], small[1], jnp.zeros((TOK - 16, TOK), F32)], axis=0).T
+def written_kernel(done, grad_query, grad_key, levels, gains):
+    grad_query[...] = done[0, :, :HD]
+    grad_key[...] = done[1, :, :HD]
+    tile = jnp.concatenate(
+        [done[0, t, HD:] for t in range(2)] + [jnp.zeros((TOK - 16, TOK), F32)], axis=0
+    ).T
     levels[...] = tile[:HEADS, :LEVELS]
-    gains[...] = small[2]
-    for copy in copies[1:]:
-        copy.wait()
+    gains[...] = done[0, 2, HD:]
 
 
 VM = pl.BlockSpec(memory_space=pltpu.VMEM)
@@ -664,9 +662,13 @@
     done = pl.pallas_call(
         whole_kernel,
         out_shape=shaped((2, HEADS, PIECE, HD)),
-        in_specs=[ANY, VM, VM, VM, ANY, ANY, SM, VM],
+        in_specs=[ANY] * 6 + [SM, ANY],
         out_specs=VM,
         scratch_shapes=[
+            pltpu.VMEM((TOK, HD), BF),
+            pltpu.VMEM((TOK, HD), BF),
+            pltpu.VMEM((HEADS, TOK), F32),
+            pltpu.VMEM((HEADS, HD), F32),
             pltpu.VMEM((HEADS * TOK, HD), BF),
             matrix,
             matrix,
@@ -690,7 +692,7 @@
             small,
             small,
             small,
-            DMA((10,)),
+            DMA((14,)),
             DMA((2, 4)),
             DMA((2, 8)),
             DMA((2, 4)),
@@ -727,9 +729,8 @@
             shaped((HEADS, LEVELS)),
             shaped((HEADS, HD)),
         ),
-        in_specs=[ANY],
-        out_specs=(ANY, ANY, VM, VM),
-        scratch_shapes=[pltpu.VMEM((3, 8, TOK), F32), DMA((3,))],
+        in_specs=[VM],
+        out_specs=(VM,) * 4,
         name="written",
     )(done)
     return grad_query, grad_key, levels, gains.reshape(-1)

time: 110 us -> 79.7 us (0.72)
  Pallas kernels: 109 us -> 78.8 us
    pallas_call x1, Pallas kernels: 33.5 us -> 2.25 us  [on_device(): pl.pallas_call(written_kernel, out_shape=(shaped((HEADS, HD, HD)), shaped...]
where the time goes in v7:
time: 79.7 us; the launch traced here: 79.5 us
  Pallas kernels  78.8 us (99%)
    pallas_call x1, Pallas kernels, on_device(): pl.pallas_call(whole_kernel, out_shape=shaped((2, HEADS, PIECE, HD)), in_...  76.6 us
    pallas_call x1, Pallas kernels, on_device(): pl.pallas_call(written_kernel, out_shape=(shaped((HEADS, HD, HD)), shaped...  2.25 us

profile of v7, /device:TPU:1, one launch (start us, length us, event | category | flops | bytes accessed | tf_op | source)
XLA Modules:
  0.0 79.5 jit_solution(12379100310313873998)
XLA Ops:
  0.6 76.6 %distill.1.done = f32[2,8,136,128]{3,2,1,0:T(8,128)} custom-call(bf16[128,1024]{1,0:T(8,128)(2,1)} %q_hbm.1, bf16[128,128]{1,0:T(8,128)(2,1)} %k_hbm.1, bf16[128,128]{1,0:T(8,128)(2,1)} %v_hbm.1, f32[8,128]{1,0:T(8,128)} %g_hbm.1, f32[8,128,128]{2,1,0:T(8,128)} %wq_hbm.1, f32[8,128,128]{2,1,0:T(8,128)} %wk_hbm.1, f32[8,13]{1,0:T(8,128)} %lw.1, f32[8,128]{1,0:T(8,128)} %bitcast.2), custom_call_target="tpu_custom_call" | custom-call | tf_op jit(solution)/shard_map/distill/pallas_call | solution.py:662
  77.2 2.3 %written.1 = (f32[8,128,128]{2,1,0:T(8,128)}, f32[8,128,128]{2,1,0:T(8,128)}, f32[8,13]{1,0:T(8,128)}, f32[8,128]{1,0:T(8,128)}) custom-call(f32[2,8,136,128]{3,2,1,0:T(8,128)} %distill.1.done), custom_call_target="tpu_custom_call" | custom-call | tf_op jit(solution)/shard_map/written/pallas_call | solution.py:724

commit v8 on v7

--- a/solution.py
+++ b/solution.py
@@ -26,7 +26,7 @@
 PIECE = 128 + 8
 LOG2E = 1.4426950408889634
 SCALE = HD**-0.5 * LOG2E
-LIMIT = 58 << 20
+LIMIT = 50 << 20
 
 
 def pieces(a):
@@ -661,7 +661,7 @@
     small = pltpu.VMEM((SMALL, TOK), F32)
     done = pl.pallas_call(
         whole_kernel,
-        out_shape=shaped((2, HEADS, PIECE, HD)),
+        out_shape=pltpu.VMEM((2, HEADS, PIECE, HD), F32),
         in_specs=[ANY] * 6 + [SM, ANY],
         out_specs=VM,
         scratch_shapes=[
@@ -732,7 +732,7 @@
         in_specs=[VM],
         out_specs=(VM,) * 4,
         name="written",
-    )(done)
+    )(pltpu.with_memory_space_constraint(done, pltpu.VMEM))
     return grad_query, grad_key, levels, gains.reshape(-1)
 
 

time: 79.7 us -> 83.2 us (1.044)
  local copies, waits for them, and re-layouts: 0 us -> 6.6 us
  Pallas kernels: 78.8 us -> 75.5 us
    unnamed x0 -> x16, local copies, waits for them, and re-layouts: none -> 6.6 us
    pallas_call x1, Pallas kernels: 76.6 us -> 74.5 us  [on_device(): pl.pallas_call(whole_kernel, out_shape=pltpu.VMEM((2, HEADS, PIECE, HD),...]
    pallas_call x1, Pallas kernels: 2.25 us -> 1.01 us  [on_device(): pl.pallas_call(written_kernel, out_shape=(shaped((HEADS, HD, HD)), shaped...]
where the time goes in v8:
time: 83.2 us; the launch traced here: 82.7 us
  Pallas kernels  75.5 us (91%)
  local copies, waits for them, and re-layouts  6.6 us (8%)
    pallas_call x1, Pallas kernels, on_device(): pl.pallas_call(whole_kernel, out_shape=pltpu.VMEM((2, HEADS, PIECE, HD),...  74.5 us
    unnamed x16, local copies, waits for them, and re-layouts  6.6 us

profile of v8, /device:TPU:1, one launch (start us, length us, event | category | flops | bytes accessed | tf_op | source)
XLA Modules:
  0.0 82.7 jit_solution(14135782944806249431)
XLA Ops:
  0.6 0.0 copy-start
  0.6 1.0 %copy-done = f32[8,128,128]{2,1,0:T(8,128)S(1)} copy-done((f32[8,128,128]{2,1,0:T(8,128)S(1)}, f32[8,128,128]{2,1,0:T(8,128)}, u32[]{:S(2)}) %copy-start) | copy-done | bytes 524312
  1.7 0.0 copy-start.1
  1.7 1.0 %copy-done.1 = f32[8,128,128]{2,1,0:T(8,128)S(1)} copy-done((f32[8,128,128]{2,1,0:T(8,128)S(1)}, f32[8,128,128]{2,1,0:T(8,128)}, u32[]{:S(2)}) %copy-start.1) | copy-done | bytes 524312
  2.7 0.0 copy-start.2
  2.7 0.9 %copy-done.2 = bf16[128,1024]{1,0:T(8,128)(2,1)S(1)} copy-done((bf16[128,1024]{1,0:T(8,128)(2,1)S(1)}, bf16[128,1024]{1,0:T(8,128)(2,1)}, u32[]{:S(2)}) %copy-start.2) | copy-done | bytes 262168
  3.7 0.0 copy-start.3
  3.7 0.8 copy-done.3
  4.4 0.0 copy-start.4
  4.4 0.8 copy-done.4
  5.2 0.0 copy-start.5
  5.2 0.7 copy-done.5
  5.9 0.0 copy-start.6
  5.9 0.7 copy-done.6
  6.6 0.0 copy-start.7
  6.6 0.7 copy-done.7
  7.2 74.5 %distill.1.done = f32[2,8,136,128]{3,2,1,0:T(8,128)S(1)} custom-call(bf16[128,1024]{1,0:T(8,128)(2,1)S(1)} %copy-done.2, bf16[128,128]{1,0:T(8,128)(2,1)S(1)} %copy-done.3, bf16[128,128]{1,0:T(8,128)(2,1)S(1)} %copy-done.4, f32[8,128]{1,0:T(8,128)S(1)} %copy-done.5, f32[8,128,128]{2,1,0:T(8,128)S(1)} %copy-done, f32[8,128,128]{2,1,0:T(8,128)S(1)} %copy-done.1, ...), custom_call_target="tpu_custom_call" | custom-call | tf_op jit(solution)/shard_map/distill/pallas_call | solution.py:662
  81.7 1.0 %written.1 = (f32[8,128,128]{2,1,0:T(8,128)}, f32[8,128,128]{2,1,0:T(8,128)}, f32[8,13]{1,0:T(8,128)}, f32[8,128]{1,0:T(8,128)}) custom-call(f32[2,8,136,128]{3,2,1,0:T(8,128)S(1)} %distill.1.done), custom_call_target="tpu_custom_call" | custom-call | tf_op jit(solution)/shard_map/written/pallas_call | solution.py:724
Async XLA Ops:
  0.6 1.0 %copy-start = (f32[8,128,128]{2,1,0:T(8,128)S(1)}, f32[8,128,128]{2,1,0:T(8,128)}, u32[]{:S(2)}) copy-start(f32[8,128,128]{2,1,0:T(8,128)} %wq_hbm.1) | copy-start | bytes 1572868
  1.7 1.0 %copy-start.1 = (f32[8,128,128]{2,1,0:T(8,128)S(1)}, f32[8,128,128]{2,1,0:T(8,128)}, u32[]{:S(2)}) copy-start(f32[8,128,128]{2,1,0:T(8,128)} %wk_hbm.1) | copy-start | bytes 1572868
  2.7 0.9 %copy-start.2 = (bf16[128,1024]{1,0:T(8,128)(2,1)S(1)}, bf16[128,1024]{1,0:T(8,128)(2,1)}, u32[]{:S(2)}) copy-start(bf16[128,1024]{1,0:T(8,128)(2,1)} %q_hbm.1) | copy-start | bytes 786436
  3.7 0.8 copy-start.3
  4.4 0.8 copy-start.4
  5.2 0.7 copy-start.5
  5.9 0.7 copy-start.6
  6.6 0.7 copy-start.7

commit v9 on v8

--- a/solution.py
+++ b/solution.py
@@ -26,7 +26,7 @@
 PIECE = 128 + 8
 LOG2E = 1.4426950408889634
 SCALE = HD**-0.5 * LOG2E
-LIMIT = 50 << 20
+LIMIT = 58 << 20
 
 
 def pieces(a):

time: 83.2 us -> 77.4 us (0.930)
  local copies, waits for them, and re-layouts: 6.6 us -> 0 us
  Pallas kernels: 75.5 us -> 76.6 us
    unnamed x16 -> x0, local copies, waits for them, and re-layouts: 6.6 us -> none
    pallas_call x1, Pallas kernels: 74.5 us -> 75.6 us  [on_device(): pl.pallas_call(whole_kernel, out_shape=pltpu.VMEM((2, HEADS, PIECE, HD),...]
where the time goes in v9:
time: 77.4 us; the launch traced here: 77.2 us
  Pallas kernels  76.6 us (99%)
    pallas_call x1, Pallas kernels, on_device(): pl.pallas_call(whole_kernel, out_shape=pltpu.VMEM((2, HEADS, PIECE, HD),...  75.6 us

profile of v9, /device:TPU:1, one launch (start us, length us, event | category | flops | bytes accessed | tf_op | source)
XLA Modules:
  0.0 77.2 jit_solution(14891081503104163799)
XLA Ops:
  0.6 75.6 %distill.1.done = f32[2,8,136,128]{3,2,1,0:T(8,128)S(1)} custom-call(bf16[128,1024]{1,0:T(8,128)(2,1)} %q_hbm.1, bf16[128,128]{1,0:T(8,128)(2,1)} %k_hbm.1, bf16[128,128]{1,0:T(8,128)(2,1)} %v_hbm.1, f32[8,128]{1,0:T(8,128)} %g_hbm.1, f32[8,128,128]{2,1,0:T(8,128)} %wq_hbm.1, f32[8,128,128]{2,1,0:T(8,128)} %wk_hbm.1, f32[8,13]{1,0:T(8,128)} %lw.1, ...), custom_call_target="tpu_custom_call" | custom-call | tf_op jit(solution)/shard_map/distill/pallas_call | solution.py:662
  76.2 1.0 %written.1 = (f32[8,128,128]{2,1,0:T(8,128)}, f32[8,128,128]{2,1,0:T(8,128)}, f32[8,13]{1,0:T(8,128)}, f32[8,128]{1,0:T(8,128)}) custom-call(f32[2,8,136,128]{3,2,1,0:T(8,128)S(1)} %distill.1.done), custom_call_target="tpu_custom_call" | custom-call | tf_op jit(solution)/shard_map/written/pallas_call | solution.py:724
